TPU v7x, 32 devices: a whole 2x2x4 slice. The times are simulated.
32 devices in a mesh: section: 2 (over x), tensor: 4 (over z), dp: 4 (over y, core).
Axes of the slice: x: 2, y: 2, z: 4, core: 2. Of those that a mesh axis runs over, the one named last changes fastest.
Arguments:
- boundary_in: bfloat16 [2, 4096, 2048], P('section', 'dp'), may hold values from -6 to 6
- segment_ids: int32 [8, 512], P('dp'), may hold values from 0 to 1, never falling along the last dimension, each value on 1 to 312 neighbouring positions
- norm_gains: bfloat16 [2, 2, 2048], P('section'), may hold values from 0.25 to 1.75
- norm_biases: bfloat16 [2, 2, 2048], P('section'), may hold values from -3 to 3
- w_qkv: bfloat16 [2, 2048, 6144], P('section', None, 'tensor'), may hold values from -0.8838835 to 0.8838835, as said below
- b_qkv: bfloat16 [2, 6144], P('section', 'tensor'), may hold values from -3 to 3
- w_out: bfloat16 [2, 2048, 2048], P('section', 'tensor'), may hold values from -0.5 to 0.5
- w_fc: bfloat16 [2, 2048, 8192], P('section', None, 'tensor'), may hold values from -0.125 to 0.125
- b_fc: bfloat16 [2, 8192], P('section', 'tensor'), may hold values from -3 to 3
- w_proj: bfloat16 [2, 8192, 2048], P('section', 'tensor'), may hold values from -0.09375 to 0.09375
- out_biases: bfloat16 [2, 2, 2048], P('section'), may hold values from -2 to 2
Outputs:
- boundary_out: float32 [2, 4096, 2048], P('section', 'dp')
- g_norm_gains: float32 [2, 2, 2048], P('section', None, ('tensor', 'dp'))
- g_norm_biases: float32 [2, 2, 2048], P('section', None, ('tensor', 'dp'))
- g_w_qkv: float32 [2, 2048, 6144], P('section', 'dp', 'tensor')
- g_b_qkv: float32 [2, 6144], P('section', ('tensor', 'dp'))
- g_w_out: float32 [2, 2048, 2048], P('section', 'tensor', 'dp')
- g_w_fc: float32 [2, 2048, 8192], P('section', 'dp', 'tensor')
- g_b_fc: float32 [2, 8192], P('section', ('tensor', 'dp'))
- g_w_proj: float32 [2, 8192, 2048], P('section', 'tensor', 'dp')
- g_out_biases: float32 [2, 2, 2048], P('section', None, 'dp')
Inputs may be any that keep to these rules, and one draw needn't show every extreme that they name: `segment_ids`: within each row of 512 tokens the ids never fall and both ids 0 and 1 occur; a document has at most 312 tokens. `w_qkv`: columns come per head in turn as 256 query, 256 key and 256 value columns.
All inputs are finite; a program needn't handle non-finite values.
Results may differ from a plain program's by a relative error of at most 0.013.
Values may be sent and summed in bfloat16 or wider, within the bound.
No kernel may reach another device: no remote copies, remote signals or barrier semaphores. Data moves between devices by JAX's collectives and lax.ppermute only.
A program may use at most 320 MiB of HBM per device.

v0:
```python
import functools

import jax
import jax.numpy as jnp
from jax import lax
from jax.experimental import pallas as pl
from jax.experimental.pallas import tpu as pltpu
from jax.sharding import PartitionSpec as P

HD = 256
ROT = 64
LANES = 128
QB = 256
FT = 512
RB = 128
EPS = 1e-05
BF = jnp.bfloat16
F32 = jnp.float32


def dot_f32(left, right, dims):
    return lax.dot_general(left, right, (dims, ((), ())), preferred_element_type=F32)


def dot(left, right):
    return dot_f32(left, right, ((1,), (0,)))


def dot_rt(left, right):
    return dot_f32(left, right, ((1,), (1,)))


def dot_lt(left, right):
    return dot_f32(left, right, ((0,), (0,)))


def rotary_tables(segments):
    length = segments.shape[0]
    places = jnp.arange(length, dtype=jnp.int32)
    starts = jnp.concatenate([jnp.ones((1,), jnp.bool_), segments[1:] != segments[:-1]])
    first_at = lax.cummax(jnp.where(starts, places, 0), axis=0)
    inside = (places - first_at).astype(F32)
    frequency = 10000.0 ** (-jnp.arange(0, ROT, 2, dtype=F32) / ROT)
    angles = inside[:, None] * frequency[None, :]
    cosine, sine = jnp.cos(angles), jnp.sin(angles)
    half = ROT // 2
    none = jnp.zeros((length, half), F32)
    rest = jnp.zeros((length, LANES - ROT), F32)
    keep = jnp.concatenate([cosine, cosine, rest + 1.0], axis=1)
    from_right = jnp.concatenate([-sine, none, rest], axis=1)
    from_left = jnp.concatenate([none, sine, rest], axis=1)
    return keep, from_right, from_left


def spin(values, keep, from_right, from_left):
    low, high = values[:, :LANES], values[:, LANES:]
    half = ROT // 2
    turned = (
        low * keep
        + pltpu.roll(low, LANES - half, 1) * from_right
        + pltpu.roll(low, half, 1) * from_left
    )
    return jnp.concatenate([turned, high], axis=1)


def spin_back(grads, keep, from_right, from_left):
    low, high = grads[:, :LANES], grads[:, LANES:]
    half = ROT // 2
    turned = (
        low * keep
        + pltpu.roll(low * from_right, half, 1)
        + pltpu.roll(low * from_left, LANES - half, 1)
    )
    return jnp.concatenate([turned, high], axis=1)


def block_scores(q, k, seg_col, seg_row, at, upto):
    raw = dot_rt(q, k) * HD ** (-0.5)
    rows = lax.broadcasted_iota(jnp.int32, raw.shape, 0) + at
    columns = lax.broadcasted_iota(jnp.int32, raw.shape, 1)
    allowed = (seg_col[at:upto] == seg_row[:, :upto]) & (rows >= columns)
    return jnp.where(allowed, raw, -1e30)


def row_stats(values):
    center = values - jnp.mean(values, axis=-1, keepdims=True)
    spread = jnp.mean(center * center, axis=-1, keepdims=True)
    inverse = lax.rsqrt(spread + EPS)
    return center * inverse, inverse


def row_blocks(length):
    return [(at, min(at + RB, length)) for at in range(0, length, RB)]


def forward_kernel(heads, with_pulled, *refs):
    (
        rows, gains, shifts, w_qkv, b_qkv, keep, from_right, from_left, seg_col, seg_row,
        w_out, w_fc, b_fc, w_proj,
    ) = refs[:14]
    refs = refs[14:]
    if with_pulled:
        pulled, refs = refs[0], refs[1:]
    n1, n2, q_out, k_out, v_out, o_out, lse_out, a_out, side_out, partial, total = refs
    step = pl.program_id(0)
    length = rows.shape[0]

    @pl.when(step == 0)
    def _():
        for at, to in row_blocks(length):
            hat, _ = row_stats(rows[at:to, :].astype(F32))
            n1[at:to, :] = (hat * gains[0:1, :] + shifts[0:1, :]).astype(BF)
            n2[at:to, :] = (hat * gains[1:2, :] + shifts[1:2, :]).astype(BF)

    @pl.when(step < heads)
    def _():
        tables = (keep[...], from_right[...], from_left[...])
        mixed = dot(n1[...], w_qkv[...]) + b_qkv[...]
        q_out[...] = spin(mixed[:, :HD], *tables).astype(BF)
        k_out[...] = spin(mixed[:, HD : 2 * HD], *tables).astype(BF)
        v_out[...] = mixed[:, 2 * HD :].astype(BF)
        for at in range(0, length, QB):
            upto = at + QB
            scores = block_scores(
                q_out[at:upto, :], k_out[:upto, :], seg_col, seg_row, at, upto
            )
            peak = jnp.max(scores, axis=-1, keepdims=True)
            raised = jnp.exp(scores - peak)
            weight = jnp.sum(raised, axis=-1, keepdims=True)
            probs = (raised / weight).astype(BF)
            o_out[at:upto, :] = dot(probs, v_out[:upto, :]).astype(BF)
            lse_out[0, at:upto, :] = peak + jnp.log(weight)
        part = dot(o_out[...], w_out[...])

        @pl.when(step == 0)
        def _():
            total[...] = part

        @pl.when(step > 0)
        def _():
            total[...] += part

    @pl.when(step >= heads)
    def _():
        for at, to in row_blocks(length):
            u = dot(n2[at:to, :], w_fc[...]) + b_fc[...]
            half_erf = 0.5 * (1.0 + lax.erf(u * 0.7071067811865476))
            a = (u * half_erf).astype(BF)
            slope = half_erf + u * jnp.exp(-0.5 * u * u) * 0.3989422804014327
            if with_pulled:
                slope = slope * pulled[at:to, :].astype(F32)
            a_out[at:to, :] = a
            side_out[at:to, :] = slope.astype(BF)
            total[at:to, :] += dot(a, w_proj[...])

    @pl.when(step == pl.num_programs(0) - 1)
    def _():
        partial[...] = total[...].astype(BF)


def fixed(shape):
    return pl.BlockSpec(shape, lambda i: (0,) * len(shape))


def forward_pass(rows, tables, seg_col, seg_row, weights, pulled):
    gains, shifts, w_qkv, b_qkv, w_out, w_fc, b_fc, w_proj = weights
    length, width = rows.shape
    heads = w_out.shape[0] // HD
    hidden = w_fc.shape[1]
    tiles = hidden // FT
    head = lambda i: jnp.minimum(i, heads - 1)
    tile = lambda i: jnp.maximum(i - heads, 0)
    by_head = lambda r, c: pl.BlockSpec((r, c), lambda i: (0, head(i)))
    by_tile = lambda r, c: pl.BlockSpec((r, c), lambda i: (0, tile(i)))
    shape = jax.ShapeDtypeStruct
    operands = [
        rows, gains, shifts, w_qkv, b_qkv[None], *tables, seg_col, seg_row, w_out, w_fc,
        b_fc[None], w_proj,
    ]
    in_specs = [
        fixed((length, width)),
        fixed((2, width)),
        fixed((2, width)),
        by_head(width, 3 * HD),
        by_head(1, 3 * HD),
        *[fixed((length, LANES))] * 3,
        fixed((length, 1)),
        fixed((1, length)),
        pl.BlockSpec((HD, width), lambda i: (head(i), 0)),
        by_tile(width, FT),
        by_tile(1, FT),
        pl.BlockSpec((FT, width), lambda i: (tile(i), 0)),
    ]
    if pulled is not None:
        operands.append(pulled)
        in_specs.append(by_tile(length, FT))
    flops = 2 * length * width * (4 * heads * HD + 2 * hidden)
    return pl.pallas_call(
        functools.partial(forward_kernel, heads, pulled is not None),
        grid=(heads + tiles,),
        in_specs=in_specs,
        out_specs=[
            fixed((length, width)),
            fixed((length, width)),
            *[by_head(length, HD)] * 4,
            pl.BlockSpec((1, length, 1), lambda i: (head(i), 0, 0)),
            by_tile(length, FT),
            by_tile(length, FT),
            fixed((length, width)),
        ],
        out_shape=[
            shape((length, width), BF),
            shape((length, width), BF),
            *[shape((length, heads * HD), BF)] * 4,
            shape((heads, length, 1), F32),
            shape((length, hidden), BF),
            shape((length, hidden), BF),
            shape((length, width), BF),
        ],
        scratch_shapes=[pltpu.VMEM((length, width), F32)],
        cost_estimate=pl.CostEstimate(
            flops=flops, bytes_accessed=2 * width * (4 * heads * HD + 2 * hidden), transcendentals=0
        ),
        compiler_params=pltpu.CompilerParams(vmem_limit_bytes=60 << 20),
    )(*operands)


def backward_kernel(heads, ready, *refs):
    (
        rows, gains, q, k, v, lse, keep, from_right, from_left, seg_col, seg_row, w_qkv,
        side, w_fc,
    ) = refs[:14]
    refs = refs[14:]
    if ready:
        d_o, refs = refs[0], refs[1:]
        error, d_mixed, sums, d_bqkv, d_bfc, one, two, dk_acc, dv_acc = refs
        d_u = None
    else:
        (
            dyb, w_out, w_proj, error, d_mixed, sums, d_bqkv, d_bfc, d_u, one, two,
            dk_acc, dv_acc,
        ) = refs
    step = pl.program_id(0)
    length = rows.shape[0]
    scale = HD ** (-0.5)

    @pl.when(step < heads)
    def _():
        tables = (keep[...], from_right[...], from_left[...])
        total_q = jnp.zeros((1, HD), F32)
        out = d_o[...] if ready else dot_rt(dyb[...], w_out[...]).astype(BF)
        dk_acc[...] = jnp.zeros_like(dk_acc)
        dv_acc[...] = jnp.zeros_like(dv_acc)
        for at in range(0, length, QB):
            upto = at + QB
            q_now, d_now = q[at:upto, :], out[at:upto]
            scores = block_scores(q_now, k[:upto, :], seg_col, seg_row, at, upto)
            probs = jnp.exp(scores - lse[0, at:upto, :])
            d_probs = dot_rt(d_now, v[:upto, :])
            row = jnp.sum(probs * d_probs, axis=-1, keepdims=True)
            d_scores = (probs * (d_probs - row)).astype(BF)
            dq = dot(d_scores, k[:upto, :]) * scale
            dq = spin_back(dq, *(t[at:upto] for t in tables)).astype(BF)
            d_mixed[at:upto, :HD] = dq
            total_q += jnp.sum(dq.astype(F32), axis=0, keepdims=True)
            dk_acc[:upto, :] += dot_lt(d_scores, q_now)
            dv_acc[:upto, :] += dot_lt(probs.astype(BF), d_now)
        dk = spin_back(dk_acc[...] * scale, *tables).astype(BF)
        d_mixed[:, HD : 2 * HD] = dk
        dv = dv_acc[...].astype(BF)
        d_mixed[:, 2 * HD :] = dv
        d_bqkv[:, :HD] = total_q
        d_bqkv[:, HD : 2 * HD] = jnp.sum(dk.astype(F32), axis=0, keepdims=True)
        d_bqkv[:, 2 * HD :] = jnp.sum(dv.astype(F32), axis=0, keepdims=True)
        part = dot_rt(d_mixed[...], w_qkv[...])

        @pl.when(step == 0)
        def _():
            one[...] = part
            two[...] = jnp.zeros_like(two)

        @pl.when(step > 0)
        def _():
            one[...] += part

    @pl.when(step >= heads)
    def _():
        bias = jnp.zeros(d_bfc.shape, F32)
        for at, to in row_blocks(length):
            if ready:
                d_now = side[at:to, :]
            else:
                d_now = dot_rt(dyb[at:to, :], w_proj[...]) * side[at:to, :].astype(F32)
                d_now = d_now.astype(BF)
                d_u[at:to, :] = d_now
            bias += jnp.sum(d_now.astype(F32), axis=0, keepdims=True)
            two[at:to, :] += dot_rt(d_now, w_fc[...])
        d_bfc[...] = bias

    @pl.when(step == pl.num_programs(0) - 1)
    def _():
        found = [jnp.zeros((1, rows.shape[1]), F32) for _ in range(4)]
        for at, to in row_blocks(length):
            hat, inverse = row_stats(rows[at:to, :].astype(F32))
            first, second = one[at:to, :], two[at:to, :]
            for i, term in enumerate((first * hat, second * hat, first, second)):
                found[i] += jnp.sum(term, axis=0, keepdims=True)
            both = first * gains[0:1, :] + second * gains[1:2, :]
            both = (
                both
                - jnp.mean(both, axis=-1, keepdims=True)
                - hat * jnp.mean(both * hat, axis=-1, keepdims=True)
            ) * inverse
            error[at:to, :] = both.astype(BF)
        for i in range(4):
            sums[i : i + 1, :] = found[i]


def backward_pass(kept, dyb, d_o, tables, seg_col, seg_row, weights):
    gains, _, w_qkv, _, w_out, w_fc, _, w_proj = weights
    rows, n1, n2, q, k, v, o, lse, a, side = kept
    ready = d_o is not None
    length, width = rows.shape
    heads = w_out.shape[0] // HD
    hidden = w_fc.shape[1]
    tiles = hidden // FT
    head = lambda i: jnp.minimum(i, heads - 1)
    tile = lambda i: jnp.maximum(i - heads, 0)
    by_head = lambda r, c: pl.BlockSpec((r, c), lambda i: (0, head(i)))
    by_tile = lambda r, c: pl.BlockSpec((r, c), lambda i: (0, tile(i)))
    shape = jax.ShapeDtypeStruct
    operands = [rows, gains, q, k, v, lse, *tables, seg_col, seg_row, w_qkv, side, w_fc]
    in_specs = [
        fixed((length, width)),
        fixed((2, width)),
        *[by_head(length, HD)] * 3,
        pl.BlockSpec((1, length, 1), lambda i: (head(i), 0, 0)),
        *[fixed((length, LANES))] * 3,
        fixed((length, 1)),
        fixed((1, length)),
        by_head(width, 3 * HD),
        by_tile(length, FT),
        by_tile(width, FT),
    ]
    out_specs = [
        fixed((length, width)),
        by_head(length, 3 * HD),
        fixed((4, width)),
        by_head(1, 3 * HD),
        by_tile(1, FT),
    ]
    out_shape = [
        shape((length, width), BF),
        shape((length, 3 * heads * HD), BF),
        shape((4, width), F32),
        shape((1, 3 * heads * HD), F32),
        shape((1, hidden), F32),
    ]
    if ready:
        operands.append(d_o)
        in_specs.append(by_head(length, HD))
    else:
        operands += [dyb, w_out, w_proj]
        in_specs += [
            fixed((length, width)),
            pl.BlockSpec((HD, width), lambda i: (head(i), 0)),
            pl.BlockSpec((FT, width), lambda i: (tile(i), 0)),
        ]
        out_specs.append(by_tile(length, FT))
        out_shape.append(shape((length, hidden), BF))
    flops = 2 * length * width * (3 * heads * HD + hidden) * (1 if ready else 2)
    result = pl.pallas_call(
        functools.partial(backward_kernel, heads, ready),
        grid=(heads + tiles,),
        in_specs=in_specs,
        out_specs=out_specs,
        out_shape=out_shape,
        scratch_shapes=[pltpu.VMEM((length, width), F32)] * 2
        + [pltpu.VMEM((length, HD), F32)] * 2,
        cost_estimate=pl.CostEstimate(
            flops=flops, bytes_accessed=2 * width * (3 * heads * HD + hidden), transcendentals=0
        ),
        compiler_params=pltpu.CompilerParams(vmem_limit_bytes=60 << 20),
    )(*operands)
    if ready:
        result = [*result, side]
    error, d_mixed, sums, d_bqkv, d_bfc, d_u = result
    return error, (n1, n2, o, a, dyb, d_u, d_mixed), (sums, d_bqkv[0], d_bfc[0])


def own_block(values, at, count):
    size = values.shape[0] // count
    return lax.dynamic_slice_in_dim(values, at * size, size, 0)


def tie(values, *earlier):
    return lax.optimization_barrier((values, earlier))[0]


def shards(
    boundary_in,
    segment_ids,
    norm_gains,
    norm_biases,
    w_qkv,
    b_qkv,
    w_out,
    w_fc,
    b_fc,
    w_proj,
    out_biases,
):
    w_qkv, w_out, w_fc, w_proj = w_qkv[0], w_out[0], w_fc[0], w_proj[0]
    b_qkv, b_fc = b_qkv[0].astype(F32), b_fc[0].astype(F32)
    gains, shifts = norm_gains[0].astype(F32), norm_biases[0].astype(F32)
    added = out_biases[0, 0].astype(F32) + out_biases[0, 1].astype(F32)
    weights = (gains, shifts, w_qkv, b_qkv, w_out, w_fc, b_fc, w_proj)
    seqs, length = segment_ids.shape
    ends = [boundary_in[0, s * length : (s + 1) * length] for s in range(seqs)]
    section = lax.axis_index("section")
    lane = lax.axis_index("tensor")
    count = lax.axis_size("tensor")
    first = section == 0
    dp = lax.axis_index("dp")
    dp_count = lax.axis_size("dp")

    tables = [rotary_tables(segment_ids[s]) for s in range(seqs)]
    columns = [segment_ids[s][:, None] for s in range(seqs)]
    lines = [segment_ids[s][None, :] for s in range(seqs)]

    def own(values):
        return own_block(values, lane, count)

    def ring(step, origin, target):
        return [(origin * count + i, target * count + (i + step) % count) for i in range(count)]

    both = ("section", "tensor")

    def scatter(partial, addend, origin):
        pieces = []
        for step in range(count):
            block = own_block(partial, (lane + step) % count, count)
            if step == 0:
                block = (block.astype(F32) + addend).astype(BF)
            pieces.append(lax.ppermute(block, both, ring(step, origin, 1 - origin)))
        return pieces

    def scatter_within(partial, addend):
        pieces = [own(partial).astype(F32) + addend]
        for step in range(1, count):
            block = own_block(partial, (lane + step) % count, count)
            route = [(i, (i + step) % count) for i in range(count)]
            pieces.append(lax.ppermute(block, "tensor", route))
        return pieces

    def summed(pieces):
        return functools.reduce(jnp.add, [p.astype(F32) for p in pieces]).astype(BF)

    def gather(block, where=None):
        size = block.shape[0]
        whole = jnp.zeros((count * size,) + block.shape[1:], block.dtype)
        for step in range(count):
            piece = block
            if step:
                if where is None:
                    route = [(i, (i + step) % count) for i in range(count)]
                    piece = lax.ppermute(block, "tensor", route)
                else:
                    piece = lax.ppermute(block, both, ring(step, where, where))
            whole = lax.dynamic_update_slice_in_dim(
                whole, piece, ((lane - step) % count) * size, 0
            )
        return whole

    def pull_back(dyb):
        return dot_rt(dyb, w_proj).astype(BF), dot_rt(dyb, w_out).astype(BF)

    def forward(rows, s, pulled=None):
        result = forward_pass(rows, tables[s], columns[s], lines[s], weights, pulled)
        return result[-1], (rows, *result[:-1])

    def backward(kept, dyb, d_o, s):
        return backward_pass(kept, dyb, d_o, tables[s], columns[s], lines[s], weights)

    def joined(left):
        return [jnp.concatenate(item, 0) for item in zip(*left)]

    def grad_block(which, joint, block):
        n1, n2, o, a, dyb, d_u, d_mixed = joint
        left, right, cut_left = (
            (a, dyb, False),
            (o, dyb, False),
            (n2, d_u, True),
            (n1, d_mixed, True),
        )[which]
        cut = left if cut_left else right
        size = cut.shape[1] // dp_count
        piece = lax.dynamic_slice_in_dim(cut, block * size, size, 1)
        return dot_lt(piece, right) if cut_left else dot_lt(left, piece)

    half_dp = dp_count // 2
    group, core = dp // 2, dp % 2
    away = [((group + g) % half_dp) * 2 + 1 - core for g in range(half_dp)]
    near = [((group + g) % half_dp) * 2 + core for g in range(half_dp)]

    def to_core(values):
        return lax.ppermute(values, "dp", [(i, i ^ 1) for i in range(dp_count)])

    def to_group(values, step):
        route = [(i, (i + 2 * step) % dp_count) for i in range(dp_count)]
        return lax.ppermute(values, "dp", route)

    early, pieces, partial = [], [], None
    for s in range(seqs):
        rows = ends[s] if s == 0 else tie(ends[s], partial)
        partial, kept = forward(rows, s)
        early.append(kept)
        addend = tie(own(ends[s]).astype(F32) + added, partial)
        pieces.append(scatter(partial, addend, 0))
    pulled = []
    for s in range(seqs):
        pulled.append(pull_back(tie(ends[s], partial, *pulled)))
    blocks = []
    for s in range(seqs):
        pieces[s][0] = tie(pieces[s][0], pulled, *blocks)
        blocks.append(summed(pieces[s]))
    inputs = [gather(block, 1) for block in blocks]
    inputs[0] = tie(inputs[0], blocks[-1])

    late_out, late, small_late, error, pieces = [], [], [], None, []
    for s in range(seqs):
        rows = inputs[s] if s == 0 else tie(inputs[s], error)
        partial, kept = forward(rows, s, pulled[s][0])
        late_out.append(partial)
        d_o = tie(pulled[s][1], partial)
        error, left, small = backward(kept, ends[s], d_o, s)
        late.append(left)
        small_late.append(small)
        pieces.append(scatter(error, tie(own(ends[s]), error).astype(F32), 1))
    pieces[0][0] = tie(pieces[0][0], error)
    blocks = [summed(pieces[0])]
    joint = joined(tie(late, blocks[-1]))

    def late_grads(joint, chosen):
        found = {}
        for which, b, index in chosen:
            found[index] = grad_block(which, joint, b).astype(BF)
            joint = tie(joint, found[index])
        return found, joint

    jobs = [(w, b, (w, "away", g)) for w in range(4) for g, b in enumerate(away)]
    jobs += [(w, b, (w, "near", g)) for w in range(4) for g, b in enumerate(near)]
    split = 3 * len(jobs) // 4
    grads_late, joint = late_grads(joint, jobs[:split])
    for s in range(1, seqs):
        pieces[s][0] = tie(pieces[s][0], joint, *blocks)
        blocks.append(summed(pieces[s]))
    more, joint = late_grads(tie(joint, blocks[-1]), jobs[split:])
    grads_late.update(more)
    returning = [gather(block, 0) for block in blocks]

    left_early, small_early, pieces, earlier = [], [], [], joint
    for s in range(seqs):
        dyb = tie(returning[s], earlier)
        error, left, small = backward(early[s], dyb, None, s)
        left_early.append(left)
        small_early.append(small)
        final = jnp.where(first, error, late_out[s])
        addend = jnp.where(
            first,
            own(returning[s]).astype(F32),
            own(inputs[s]).astype(F32) + added,
        )
        pieces.append(scatter_within(final, addend))
        earlier = final
    joint = joined(tie(left_early, earlier))

    def chosen(which, block, kept):
        return jnp.where(first, grad_block(which, joint, block), kept.astype(F32))

    arrived = []
    for w in range(4):
        sent = jnp.stack(
            [
                chosen(w, b, grads_late[w, "away", g]).astype(BF)
                for g, b in enumerate(away)
            ]
        )
        arrived.append(to_core(sent))
        joint = tie(joint, sent)
    received = []
    for w in range(4):
        others = []
        for g in range(1, half_dp):
            part = chosen(w, near[g], grads_late[w, "near", g])
            part = (part + arrived[w][g].astype(F32)).astype(BF)
            joint = tie(joint, part)
            others.append(to_group(part, g))
        received.append(others)
    mine = []
    for w in range(4):
        part = chosen(w, near[0], grads_late[w, "near", 0])
        mine.append(part + arrived[w][0].astype(F32))
        joint = tie(joint, mine[-1])

    small = [
        jnp.where(first, functools.reduce(jnp.add, x), functools.reduce(jnp.add, y))
        for x, y in zip(zip(*small_early), zip(*small_late))
    ]
    d_norm, d_bqkv, d_bfc = small
    outb = [
        jnp.sum(jnp.where(first, returning[s], ends[s]).astype(F32), axis=0)
        for s in range(seqs)
    ]
    outb = functools.reduce(jnp.add, outb)
    cut = d_norm.shape[1] // count
    d_norm = d_norm.reshape(4, count, cut).swapaxes(0, 1)
    got = lax.dynamic_index_in_dim(d_norm, lane, 0, keepdims=False)
    for step in range(1, count):
        block = lax.dynamic_index_in_dim(d_norm, (lane + step) % count, 0, keepdims=False)
        route = [(i, (i + step) % count) for i in range(count)]
        got = got + lax.ppermute(block, "tensor", route)
    packed = [got, d_bqkv[None], d_bfc[None], outb[None]]
    packed = [
        x.reshape(x.shape[0], dp_count, -1).swapaxes(0, 1).reshape(dp_count, -1) for x in packed
    ]
    sizes = [x.shape[1] for x in packed]
    packed = jnp.concatenate(packed, axis=1)
    small = lax.dynamic_index_in_dim(packed, dp, 0, keepdims=True)
    for step in range(1, dp_count):
        block = lax.dynamic_index_in_dim(packed, (dp + step) % dp_count, 0, keepdims=True)
        route = [(i, (i + step) % dp_count) for i in range(dp_count)]
        small = small + lax.ppermute(block, "dp", route)
    edges = [sum(sizes[:i]) for i in range(len(sizes) + 1)]
    g_norm, g_bqkv, g_bfc, g_outb = [
        small[0, edges[i] : edges[i + 1]] for i in range(len(sizes))
    ]
    g_norm = g_norm.reshape(4, -1)

    results, earlier = [], mine
    for s in range(seqs):
        pieces[s][0] = tie(pieces[s][0], earlier)
        block = summed(pieces[s])
        results.append(gather(block))
        earlier = block
    g_proj, g_out, g_fc, g_qkv = [
        functools.reduce(jnp.add, [x.astype(F32) for x in others], part)
        for part, others in zip(mine, received)
    ]
    boundary_out = jnp.concatenate(results, 0).astype(F32)[None]
    return (
        boundary_out,
        g_norm[None, :2],
        g_norm[None, 2:],
        g_qkv[None],
        g_bqkv[None],
        g_out[None],
        g_fc[None],
        g_bfc[None],
        g_proj[None],
        jnp.stack([g_outb, g_outb])[None],
    )


def solution(mesh):
    step = build(mesh)
    return step


def build(mesh):
    return jax.shard_map(
        shards,
        mesh=mesh,
        in_specs=(
            P("section", "dp", None),
            P("dp", None),
            P("section", None, None),
            P("section", None, None),
            P("section", None, "tensor"),
            P("section", "tensor"),
            P("section", "tensor", None),
            P("section", None, "tensor"),
            P("section", "tensor"),
            P("section", "tensor", None),
            P("section", None, None),
        ),
        out_specs=(
            P("section", "dp", None),
            P("section", None, ("tensor", "dp")),
            P("section", None, ("tensor", "dp")),
            P("section", "dp", "tensor"),
            P("section", ("tensor", "dp")),
            P("section", "tensor", "dp"),
            P("section", "dp", "tensor"),
            P("section", ("tensor", "dp")),
            P("section", "tensor", "dp"),
            P("section", None, "dp"),
        ),
        check_vma=False,
    )
```

profile of v0, /device:TPU:0, one launch (start us, length us, event | category | flops | bytes accessed | tf_op | source)
XLA Modules:
  0.0 889.6 jit_solution(14091983929157684867)
XLA Ops:
  19.9 31.9 %shard_map.186 = (bf16[512,2048]{1,0:T(8,128)(2,1)}, bf16[512,2048]{1,0:T(8,128)(2,1)}, bf16[512,512]{1,0:T(8,128)(2,1)}, bf16[512,512]{1,0:T(8,128)(2,1)}, bf16...) custom-call(bf16[512,2048]{1,0:T(8,128)(2,1)} %get-tuple-element.346, ...), custom_call_target="tpu_custom_call" | custom-call | flops 12884901888 | bytes 25165824 | tf_op jit(solution)/shard_map/pallas_call | solution.py:198
  69.9 32.0 %shard_map.187 = (bf16[512,2048]{1,0:T(8,128)(2,1)}, bf16[512,2048]{1,0:T(8,128)(2,1)}, bf16[512,512]{1,0:T(8,128)(2,1)}, bf16[512,512]{1,0:T(8,128)(2,1)}, bf16...) custom-call(bf16[512,2048]{1,0:T(8,128)(2,1)} %get-tuple-element.347, ...), custom_call_target="tpu_custom_call" | custom-call | flops 12884901888 | bytes 25165824 | tf_op jit(solution)/shard_map/pallas_call | solution.py:198
  106.5 9.5 %convolution_convert_fusion.13.refs_14_ = bf16[512,2048]{1,0:T(8,128)(2,1)} fusion(bf16[512,2048]{1,0:T(8,128)(2,1)S(1)} %copy-done.13, bf16[1,2048,2048]{2,1,0:T(8,128)(2,1)} %param.20), kind=kOutput, calls=%fused_computation.49 | convolution fusion | flops 4296015872 | bytes 12582912 | tf_op jit(solution)/shard_map/dot_general | solution.py:22
  143.4 11.0 %collective-permute-done.8 = bf16[128,2048]{1,0:T(8,128)(2,1)S(1)} collective-permute-done((bf16[128,2048]{1,0:T(8,128)(2,1)S(1)}, bf16[128,2048]{1,0:T(8,128)(2,1)S(1)}, u32[]{:S(2)}, u32[]{:S(2)}) %collective-permute-start.8) | collective-permute-done | bytes 524320 | tf_op jit(solution)/shard_map/ppermute | solution.py:445
  154.4 10.1 %collective-permute-done.9 = bf16[128,2048]{1,0:T(8,128)(2,1)S(1)} collective-permute-done((bf16[128,2048]{1,0:T(8,128)(2,1)S(1)}, bf16[128,2048]{1,0:T(8,128)(2,1)S(1)}, u32[]{:S(2)}, u32[]{:S(2)}) %collective-permute-start.9) | collective-permute-done | bytes 524320 | tf_op jit(solution)/shard_map/ppermute | solution.py:445
  172.2 32.2 %shard_map.188 = (bf16[512,2048]{1,0:T(8,128)(2,1)}, bf16[512,2048]{1,0:T(8,128)(2,1)}, bf16[512,512]{1,0:T(8,128)(2,1)}, bf16[512,512]{1,0:T(8,128)(2,1)}, bf16...) custom-call(bf16[512,2048]{1,0:T(8,128)(2,1)} %copy-done.18, ...), custom_call_target="tpu_custom_call" | custom-call | flops 12884901888 | bytes 25165824 | tf_op jit(solution)/shard_map/pallas_call | solution.py:198
  204.5 29.5 %shard_map.189 = (bf16[512,2048]{1,0:T(8,128)(2,1)}, bf16[512,1536]{1,0:T(8,128)(2,1)}, f32[4,2048]{1,0:T(4,128)}, f32[1,1536]{1,0:T(1,128)}, f32[1,2048]{1,0:T(1,128)}) custom-call(bf16[512,2048]{1,0:T(8,128)(2,1)} %copy-done.18, f32[2,2048]{1,0:T(2,128)} %get-tuple-element.633.refs_1_, bf16[512,512]{1,0:T(8,128)(2,1)} %get-tuple-element.297.refs_2_, ...), custom_call_target="tpu_custom_call" | custom-call | flops 7516192768 | bytes 14680064 | tf_op jit(solution)/shard_map/pallas_call | solution.py:372
  242.1 32.4 %shard_map.190 = (bf16[512,2048]{1,0:T(8,128)(2,1)}, bf16[512,2048]{1,0:T(8,128)(2,1)}, bf16[512,512]{1,0:T(8,128)(2,1)}, bf16[512,512]{1,0:T(8,128)(2,1)}, bf16...) custom-call(bf16[512,2048]{1,0:T(8,128)(2,1)} %copy-done.21, ...), custom_call_target="tpu_custom_call" | custom-call | flops 12884901888 | bytes 25165824 | tf_op jit(solution)/shard_map/pallas_call | solution.py:198
  278.5 29.4 %shard_map.191 = (bf16[512,2048]{1,0:T(8,128)(2,1)}, bf16[512,1536]{1,0:T(8,128)(2,1)}, f32[4,2048]{1,0:T(4,128)}, f32[1,1536]{1,0:T(1,128)}, f32[1,2048]{1,0:T(1,128)}) custom-call(bf16[512,2048]{1,0:T(8,128)(2,1)} %copy-done.21, f32[2,2048]{1,0:T(2,128)} %get-tuple-element.633.refs_1_, bf16[512,512]{1,0:T(8,128)(2,1)} %get-tuple-element.307.refs_2_, ...), custom_call_target="tpu_custom_call" | custom-call | flops 7516192768 | bytes 14680064 | tf_op jit(solution)/shard_map/pallas_call | solution.py:372
  314.7 16.8 %collective-permute-done.16 = bf16[128,2048]{1,0:T(8,128)(2,1)S(1)} collective-permute-done((bf16[128,2048]{1,0:T(8,128)(2,1)S(1)}, bf16[128,2048]{1,0:T(8,128)(2,1)S(1)}, u32[]{:S(2)}, u32[]{:S(2)}) %collective-permute-start.16) | collective-permute-done | bytes 524320 | tf_op jit(solution)/shard_map/ppermute | solution.py:445
  335.9 35.7 %collective-permute-start.18 = (bf16[128,2048]{1,0:T(8,128)(2,1)}, bf16[128,2048]{1,0:T(8,128)(2,1)S(1)}, u32[]{:S(2)}, u32[]{:S(2)}) collective-permute-start(bf16[128,2048]{1,0:T(8,128)(2,1)} %get-tuple-element.563), channel_id=1, source_target_pairs={{0,4},{4,8},{8,12},{12,0},{1,5},{5,9},{9,13},{13,1},{2,6},{6,10},{... | collective-permute-start | bytes 1572872 | tf_op jit(solution)/shard_map/ppermute | solution.py:469
  465.0 7.3 collective-permute-done.20
  473.7 45.9 %shard_map.192 = (bf16[512,2048]{1,0:T(8,128)(2,1)}, bf16[512,1536]{1,0:T(8,128)(2,1)}, f32[4,2048]{1,0:T(4,128)}, f32[1,1536]{1,0:T(1,128)}, f32[1,2048]{1,0:T(1,128)}, /*index=5*/bf16[512,2048]{1,0:T(8,128)(2,1)}) custom-call(bf16[512,2048]{1,0:T(8,128)(2,1)} %get-tuple-element.346.refs_0_, f32[2,2048]{1,0:T(2,128)} %get-tuple-element.633.refs_1_, ...), custom_call_target="tpu_custom_call" | custom-call | flops 15032385536 | bytes 14680064 | tf_op jit(solution)/shard_map/pallas_call | solution.py:372
  526.4 46.1 %shard_map.193 = (bf16[512,2048]{1,0:T(8,128)(2,1)}, bf16[512,1536]{1,0:T(8,128)(2,1)}, f32[4,2048]{1,0:T(4,128)}, f32[1,1536]{1,0:T(1,128)}, f32[1,2048]{1,0:T(1,128)}, /*index=5*/bf16[512,2048]{1,0:T(8,128)(2,1)}) custom-call(bf16[512,2048]{1,0:T(8,128)(2,1)} %get-tuple-element.347.refs_0_, f32[2,2048]{1,0:T(2,128)} %get-tuple-element.633.refs_1_, ...), custom_call_target="tpu_custom_call" | custom-call | flops 15032385536 | bytes 14680064 | tf_op jit(solution)/shard_map/pallas_call | solution.py:372
  621.5 20.9 %collective-permute-start.44 = (f32[4,512]{1,0:T(4,128)S(1)}, f32[4,512]{1,0:T(4,128)S(1)}, u32[]{:S(2)}, u32[]{:S(2)}) collective-permute-start(f32[4,512]{1,0:T(4,128)S(1)} %bitcast.198), channel_id=1, source_target_pairs={{0,4},{4,8},{8,12},{12,0},{1,5},{5,9},{9,13},{13,1},{2,6},{6,10},{... | collective-permute-start | bytes 24584 | tf_op jit(solution)/shard_map/ppermute | solution.py:622
  673.5 6.8 fusion.1
  718.9 24.8 %collective-permute-start.53 = (bf16[2048,512]{1,0:T(8,128)(2,1)}, bf16[2048,512]{1,0:T(8,128)(2,1)S(1)}, u32[]{:S(2)}, u32[]{:S(2)}) collective-permute-start(bf16[2048,512]{1,0:T(8,128)(2,1)} %fusion.1), channel_id=1, source_target_pairs={{0,2},{1,3},{2,0},{3,1},{4,6},{5,7},{6,4},{7,5},{8,10},{9,11},{10,... | collective-permute-start | bytes 6291464 | tf_op jit(solution)/shard_map/ppermute | solution.py:511
  753.7 7.1 collective-permute-start.35
  765.9 10.5 %collective-permute-done.35 = bf16[128,2048]{1,0:T(8,128)(2,1)S(1)} collective-permute-done((bf16[128,2048]{1,0:T(8,128)(2,1)S(1)}, bf16[128,2048]{1,0:T(8,128)(2,1)S(1)}, u32[]{:S(2)}, u32[]{:S(2)}) %collective-permute-start.35) | collective-permute-done | bytes 524320 | tf_op jit(solution)/shard_map/ppermute | solution.py:467
  779.2 19.5 %collective-permute-done.36 = bf16[128,2048]{1,0:T(8,128)(2,1)S(1)} collective-permute-done((bf16[128,2048]{1,0:T(8,128)(2,1)S(1)}, bf16[128,2048]{1,0:T(8,128)(2,1)S(1)}, u32[]{:S(2)}, u32[]{:S(2)}) %collective-permute-start.36) | collective-permute-done | bytes 524320 | tf_op jit(solution)/shard_map/ppermute | solution.py:467
  798.6 8.2 collective-permute-start.41
  810.4 12.1 %collective-permute-done.41 = bf16[128,2048]{1,0:T(8,128)(2,1)S(1)} collective-permute-done((bf16[128,2048]{1,0:T(8,128)(2,1)S(1)}, bf16[128,2048]{1,0:T(8,128)(2,1)S(1)}, u32[]{:S(2)}, u32[]{:S(2)}) %collective-permute-start.41) | collective-permute-done | bytes 524320 | tf_op jit(solution)/shard_map/ppermute | solution.py:467
  825.0 19.5 %collective-permute-done.42 = bf16[128,2048]{1,0:T(8,128)(2,1)S(1)} collective-permute-done((bf16[128,2048]{1,0:T(8,128)(2,1)S(1)}, bf16[128,2048]{1,0:T(8,128)(2,1)S(1)}, u32[]{:S(2)}, u32[]{:S(2)}) %collective-permute-start.42) | collective-permute-done | bytes 524320 | tf_op jit(solution)/shard_map/ppermute | solution.py:467
  853.9 27.7 %collective-permute-done.50 = bf16[512,1536]{1,0:T(8,128)(2,1)S(1)} collective-permute-done((bf16[512,1536]{1,0:T(8,128)(2,1)S(1)}, bf16[512,1536]{1,0:T(8,128)(2,1)S(1)}, u32[]{:S(2)}, u32[]{:S(2)}) %collective-permute-start.50) | collective-permute-done | bytes 1572896 | tf_op jit(solution)/shard_map/ppermute | solution.py:511
  (467 shorter events, 359.7 us)
Async XLA Ops:
  53.7 75.4 %collective-permute-start = (bf16[128,2048]{1,0:T(8,128)(2,1)}, bf16[128,2048]{1,0:T(8,128)(2,1)}, u32[]{:S(2)}, u32[]{:S(2)}) collective-permute-start(bf16[128,2048]{1,0:T(8,128)(2,1)} %add_convert_fusion.9), channel_id=1, source_target_pairs={{0,16},{4,20},{8,24},{12,28},{1,17},{5,21},{9,25},{13,29},{2,18},{... | collective-permute-start | bytes 1572872 | tf_op jit(solution)/shard_map/ppermute | solution.py:445
  62.1 68.4 %collective-permute-start.1 = (bf16[128,2048]{1,0:T(8,128)(2,1)}, bf16[128,2048]{1,0:T(8,128)(2,1)}, u32[]{:S(2)}, u32[]{:S(2)}) collective-permute-start(bf16[128,2048]{1,0:T(8,128)(2,1)} %get-tuple-element.590), channel_id=1, source_target_pairs={{0,20},{4,24},{8,28},{12,16},{1,21},{5,25},{9,29},{13,17},{2,22},{... | collective-permute-start | bytes 1572872 | tf_op jit(solution)/shard_map/ppermute | solution.py:445
  64.4 67.4 %collective-permute-start.2 = (bf16[128,2048]{1,0:T(8,128)(2,1)}, bf16[128,2048]{1,0:T(8,128)(2,1)}, u32[]{:S(2)}, u32[]{:S(2)}) collective-permute-start(bf16[128,2048]{1,0:T(8,128)(2,1)} %get-tuple-element.592), channel_id=1, source_target_pairs={{0,24},{4,28},{8,16},{12,20},{1,25},{5,29},{9,17},{13,21},{2,26},{... | collective-permute-start | bytes 1572872 | tf_op jit(solution)/shard_map/ppermute | solution.py:445
  66.8 66.4 %collective-permute-start.3 = (bf16[128,2048]{1,0:T(8,128)(2,1)}, bf16[128,2048]{1,0:T(8,128)(2,1)}, u32[]{:S(2)}, u32[]{:S(2)}) collective-permute-start(bf16[128,2048]{1,0:T(8,128)(2,1)} %get-tuple-element.591), channel_id=1, source_target_pairs={{0,28},{4,16},{8,20},{12,24},{1,29},{5,17},{9,21},{13,25},{2,30},{... | collective-permute-start | bytes 1572872 | tf_op jit(solution)/shard_map/ppermute | solution.py:445
  166.9 70.5 %collective-permute-start.12 = (bf16[128,2048]{1,0:T(8,128)(2,1)}, bf16[128,2048]{1,0:T(8,128)(2,1)}, u32[]{:S(2)}, u32[]{:S(2)}) collective-permute-start(bf16[128,2048]{1,0:T(8,128)(2,1)} %get-tuple-element.569), channel_id=1, source_target_pairs={{16,20},{20,24},{24,28},{28,16},{17,21},{21,25},{25,29},{29,17},{1... | collective-permute-start | bytes 1572872 | tf_op jit(solution)/shard_map/ppermute | solution.py:469
  168.4 70.2 %collective-permute-start.13 = (bf16[128,2048]{1,0:T(8,128)(2,1)}, bf16[128,2048]{1,0:T(8,128)(2,1)S(1)}, u32[]{:S(2)}, u32[]{:S(2)}) collective-permute-start(bf16[128,2048]{1,0:T(8,128)(2,1)} %get-tuple-element.569), channel_id=1, source_target_pairs={{16,24},{20,28},{24,16},{28,20},{17,25},{21,29},{25,17},{29,21},{1... | collective-permute-start | bytes 1572872 | tf_op jit(solution)/shard_map/ppermute | solution.py:469
  169.1 70.5 %collective-permute-start.14 = (bf16[128,2048]{1,0:T(8,128)(2,1)}, bf16[128,2048]{1,0:T(8,128)(2,1)}, u32[]{:S(2)}, u32[]{:S(2)}) collective-permute-start(bf16[128,2048]{1,0:T(8,128)(2,1)} %get-tuple-element.569), channel_id=1, source_target_pairs={{16,28},{20,16},{24,20},{28,24},{17,29},{21,17},{25,21},{29,25},{1... | collective-permute-start | bytes 1572872 | tf_op jit(solution)/shard_map/ppermute | solution.py:469
  236.1 75.8 %collective-permute-start.11 = (bf16[128,2048]{1,0:T(8,128)(2,1)}, bf16[128,2048]{1,0:T(8,128)(2,1)}, u32[]{:S(2)}, u32[]{:S(2)}) collective-permute-start(bf16[128,2048]{1,0:T(8,128)(2,1)} %add_convert_fusion.5), channel_id=1, source_target_pairs={{16,0},{20,4},{24,8},{28,12},{17,1},{21,5},{25,9},{29,13},{18,2},{... | collective-permute-start | bytes 1572872 | tf_op jit(solution)/shard_map/ppermute | solution.py:445
  277.2 55.6 %collective-permute-start.17 = (bf16[128,2048]{1,0:T(8,128)(2,1)S(1)}, bf16[128,2048]{1,0:T(8,128)(2,1)}, u32[]{:S(2)}, u32[]{:S(2)}) collective-permute-start(bf16[128,2048]{1,0:T(8,128)(2,1)S(1)} %get-tuple-element.585), channel_id=1, source_target_pairs={{16,12},{20,0},{24,4},{28,8},{17,13},{21,1},{25,5},{29,9},{18,14},... | collective-permute-start | bytes 1572872 | tf_op jit(solution)/shard_map/ppermute | solution.py:445
  309.1 122.3 %collective-permute-start.21 = (bf16[128,2048]{1,0:T(8,128)(2,1)S(1)}, bf16[128,2048]{1,0:T(8,128)(2,1)S(1)}, u32[]{:S(2)}, u32[]{:S(2)}) collective-permute-start(bf16[128,2048]{1,0:T(8,128)(2,1)S(1)} %add_convert_fusion.3), channel_id=1, source_target_pairs={{16,0},{20,4},{24,8},{28,12},{17,1},{21,5},{25,9},{29,13},{18,2},{... | collective-permute-start | bytes 1572872 | tf_op jit(solution)/shard_map/ppermute | solution.py:445
  312.0 121.4 %collective-permute-start.22 = (bf16[128,2048]{1,0:T(8,128)(2,1)S(1)}, bf16[128,2048]{1,0:T(8,128)(2,1)}, u32[]{:S(2)}, u32[]{:S(2)}) collective-permute-start(bf16[128,2048]{1,0:T(8,128)(2,1)S(1)} %get-tuple-element.587), channel_id=1, source_target_pairs={{16,4},{20,8},{24,12},{28,0},{17,5},{21,9},{25,13},{29,1},{18,6},{... | collective-permute-start | bytes 1572872 | tf_op jit(solution)/shard_map/ppermute | solution.py:445
  313.4 124.2 %collective-permute-start.23 = (bf16[128,2048]{1,0:T(8,128)(2,1)S(1)}, bf16[128,2048]{1,0:T(8,128)(2,1)}, u32[]{:S(2)}, u32[]{:S(2)}) collective-permute-start(bf16[128,2048]{1,0:T(8,128)(2,1)S(1)} %get-tuple-element.589), channel_id=1, source_target_pairs={{16,8},{20,12},{24,0},{28,4},{17,9},{21,13},{25,1},{29,5},{18,10},... | collective-permute-start | bytes 1572872 | tf_op jit(solution)/shard_map/ppermute | solution.py:445
  331.5 106.1 %collective-permute-start.24 = (bf16[128,2048]{1,0:T(8,128)(2,1)S(1)}, bf16[128,2048]{1,0:T(8,128)(2,1)}, u32[]{:S(2)}, u32[]{:S(2)}) collective-permute-start(bf16[128,2048]{1,0:T(8,128)(2,1)S(1)} %get-tuple-element.588), channel_id=1, source_target_pairs={{16,12},{20,0},{24,4},{28,8},{17,13},{21,1},{25,5},{29,9},{18,14},... | collective-permute-start | bytes 1572872 | tf_op jit(solution)/shard_map/ppermute | solution.py:445
  335.9 125.7 %collective-permute-start.18 = (bf16[128,2048]{1,0:T(8,128)(2,1)}, bf16[128,2048]{1,0:T(8,128)(2,1)S(1)}, u32[]{:S(2)}, u32[]{:S(2)}) collective-permute-start(bf16[128,2048]{1,0:T(8,128)(2,1)} %get-tuple-element.563), channel_id=1, source_target_pairs={{0,4},{4,8},{8,12},{12,0},{1,5},{5,9},{9,13},{13,1},{2,6},{6,10},{... | collective-permute-start | bytes 1572872 | tf_op jit(solution)/shard_map/ppermute | solution.py:469
  441.9 77.7 %collective-permute-start.25 = (bf16[128,2048]{1,0:T(8,128)(2,1)}, bf16[128,2048]{1,0:T(8,128)(2,1)S(1)}, u32[]{:S(2)}, u32[]{:S(2)}) collective-permute-start(bf16[128,2048]{1,0:T(8,128)(2,1)} %get-tuple-element.565), channel_id=1, source_target_pairs={{0,4},{4,8},{8,12},{12,0},{1,5},{5,9},{9,13},{13,1},{2,6},{6,10},{... | collective-permute-start | bytes 1572872 | tf_op jit(solution)/shard_map/ppermute | solution.py:469
  443.8 76.7 %collective-permute-start.26 = (bf16[128,2048]{1,0:T(8,128)(2,1)}, bf16[128,2048]{1,0:T(8,128)(2,1)S(1)}, u32[]{:S(2)}, u32[]{:S(2)}) collective-permute-start(bf16[128,2048]{1,0:T(8,128)(2,1)} %get-tuple-element.565), channel_id=1, source_target_pairs={{0,8},{4,12},{8,0},{12,4},{1,9},{5,13},{9,1},{13,5},{2,10},{6,14},... | collective-permute-start | bytes 1572872 | tf_op jit(solution)/shard_map/ppermute | solution.py:469
  461.7 62.9 %collective-permute-start.27 = (bf16[128,2048]{1,0:T(8,128)(2,1)}, bf16[128,2048]{1,0:T(8,128)(2,1)}, u32[]{:S(2)}, u32[]{:S(2)}) collective-permute-start(bf16[128,2048]{1,0:T(8,128)(2,1)} %get-tuple-element.565), channel_id=1, source_target_pairs={{0,12},{4,0},{8,4},{12,8},{1,13},{5,1},{9,5},{13,9},{2,14},{6,2},{... | collective-permute-start | bytes 1572872 | tf_op jit(solution)/shard_map/ppermute | solution.py:469
  620.8 62.5 %collective-permute-start.30 = (bf16[2,512,2048]{2,1,0:T(8,128)(2,1)}, bf16[2,512,2048]{2,1,0:T(8,128)(2,1)}, u32[]{:S(2)}, u32[]{:S(2)}) collective-permute-start(bf16[2,512,2048]{2,1,0:T(8,128)(2,1)} %pad_maximum_fusion.7), channel_id=1, source_target_pairs={{0,1},{1,0},{2,3},{3,2},{4,5},{5,4},{6,7},{7,6},{8,9},{9,8},{10,11... | collective-permute-start | bytes 12582920 | tf_op jit(solution)/shard_map/ppermute | solution.py:507
  680.3 63.5 %collective-permute-start.34 = (bf16[128,2048]{1,0:T(8,128)(2,1)}, bf16[128,2048]{1,0:T(8,128)(2,1)}, u32[]{:S(2)}, u32[]{:S(2)}) collective-permute-start(bf16[128,2048]{1,0:T(8,128)(2,1)} %get-tuple-element.582), channel_id=1, source_target_pairs={{0,12},{4,0},{8,4},{12,8},{1,13},{5,1},{9,5},{13,9},{2,14},{6,2},{... | collective-permute-start | bytes 1572872 | tf_op jit(solution)/shard_map/ppermute | solution.py:453
  683.3 68.4 %collective-permute-start.38 = (bf16[128,2048]{1,0:T(8,128)(2,1)}, bf16[128,2048]{1,0:T(8,128)(2,1)}, u32[]{:S(2)}, u32[]{:S(2)}) collective-permute-start(bf16[128,2048]{1,0:T(8,128)(2,1)} %get-tuple-element.578), channel_id=1, source_target_pairs={{0,4},{4,8},{8,12},{12,0},{1,5},{5,9},{9,13},{13,1},{2,6},{6,10},{... | collective-permute-start | bytes 1572872 | tf_op jit(solution)/shard_map/ppermute | solution.py:453
  691.8 61.9 %collective-permute-start.39 = (bf16[128,2048]{1,0:T(8,128)(2,1)}, bf16[128,2048]{1,0:T(8,128)(2,1)S(1)}, u32[]{:S(2)}, u32[]{:S(2)}) collective-permute-start(bf16[128,2048]{1,0:T(8,128)(2,1)} %get-tuple-element.580), channel_id=1, source_target_pairs={{0,8},{4,12},{8,0},{12,4},{1,9},{5,13},{9,1},{13,5},{2,10},{6,14},... | collective-permute-start | bytes 1572872 | tf_op jit(solution)/shard_map/ppermute | solution.py:453
  718.9 164.8 %collective-permute-start.53 = (bf16[2048,512]{1,0:T(8,128)(2,1)}, bf16[2048,512]{1,0:T(8,128)(2,1)S(1)}, u32[]{:S(2)}, u32[]{:S(2)}) collective-permute-start(bf16[2048,512]{1,0:T(8,128)(2,1)} %fusion.1), channel_id=1, source_target_pairs={{0,2},{1,3},{2,0},{3,1},{4,6},{5,7},{6,4},{7,5},{8,10},{9,11},{10,... | collective-permute-start | bytes 6291464 | tf_op jit(solution)/shard_map/ppermute | solution.py:511
  743.8 142.7 %collective-permute-start.52 = (bf16[512,2048]{1,0:T(8,128)(2,1)}, bf16[512,2048]{1,0:T(8,128)(2,1)S(1)}, u32[]{:S(2)}, u32[]{:S(2)}) collective-permute-start(bf16[512,2048]{1,0:T(8,128)(2,1)} %fusion), channel_id=1, source_target_pairs={{0,2},{1,3},{2,0},{3,1},{4,6},{5,7},{6,4},{7,5},{8,10},{9,11},{10,... | collective-permute-start | bytes 6291464 | tf_op jit(solution)/shard_map/ppermute | solution.py:511
  751.8 96.7 %collective-permute-start.51 = (bf16[512,512]{1,0:T(8,128)(2,1)S(1)}, bf16[512,512]{1,0:T(8,128)(2,1)S(1)}, u32[]{:S(2)}, u32[]{:S(2)}) collective-permute-start(bf16[512,512]{1,0:T(8,128)(2,1)S(1)} %copy-done.95), channel_id=1, source_target_pairs={{0,2},{1,3},{2,0},{3,1},{4,6},{5,7},{6,4},{7,5},{8,10},{9,11},{10,... | collective-permute-start | bytes 1572872 | tf_op jit(solution)/shard_map/ppermute | solution.py:511
  (137 other events, 1922.2 us)
where the time goes:
time: 899 us; the launch traced here: 890 us
  Pallas kernels  279 us (31%)
  starting transfers between devices  197 us (22%)
  waiting for transfers between devices  144 us (16%)
  matrix products  125 us (14%)
  other arithmetic  71.5 us (8%)
  local copies, waits for them, and re-layouts  70.2 us (8%)
    pallas_call x4, Pallas kernels, backward_pass(): pl.pallas_call(functools.partial(backward_kernel, heads, ready), grid=(he...  151 us
    pallas_call x4, Pallas kernels, forward_pass(): pl.pallas_call(functools.partial(forward_kernel, heads, pulled is not Non...  129 us
    dot_general x36, matrix products, dot_f32(): lax.dot_general(left, right, (dims, ((), ())), preferred_element_type=F32)  125 us
    ppermute x6, waiting for transfers between devices, gather(): piece = lax.ppermute(block, 'tensor', route)  62.3 us
    ppermute x12, starting transfers between devices, gather(): piece = lax.ppermute(block, both, ring(step, where, where))  57.1 us
    ppermute x16, waiting for transfers between devices, scatter(): pieces.append(lax.ppermute(block, both, ring(step, origin, 1 - origin)))  43.9 us
    unnamed x224, local copies, waits for them, and re-layouts  35.1 us
    ppermute x4, starting transfers between devices, to_group(): return lax.ppermute(values, 'dp', route)  34 us
  transfers between devices with their start and end apart: 54, of which 13 were waited for; matrix products, arithmetic and copies ran while one was open for 20% of the time, Pallas kernels for 23%

commit v1 on v0

v1 whole, which is shorter than its diff:
```python
import functools

import jax
import jax.numpy as jnp
from jax import lax
from jax.experimental import pallas as pl
from jax.experimental.pallas import tpu as pltpu
from jax.sharding import PartitionSpec as P

HD = 256
ROT = 64
LANES = 128
QB = 256
FT = 512
RB = 512
LB = 128
EPS = 1e-05
BF = jnp.bfloat16
F32 = jnp.float32


def dot_f32(left, right, dims):
    return lax.dot_general(left, right, (dims, ((), ())), preferred_element_type=F32)


def dot(left, right):
    return dot_f32(left, right, ((1,), (0,)))


def dot_rt(left, right):
    return dot_f32(left, right, ((1,), (1,)))


def dot_lt(left, right):
    return dot_f32(left, right, ((0,), (0,)))


def rotary_tables(segments):
    seqs, length = segments.shape
    places = jnp.arange(length, dtype=jnp.int32)
    same = segments[:, :, None] == segments[:, None, :]
    earlier = same & (places[:, None] < places[None, :])[None]
    inside = jnp.sum(earlier.astype(F32), axis=1)
    frequency = 10000.0 ** (-jnp.arange(0, ROT, 2, dtype=F32) / ROT)
    angles = frequency[None, :, None] * inside[:, None, :]
    cosine, sine = jnp.cos(angles), jnp.sin(angles)
    none = jnp.zeros_like(sine)
    rest = jnp.zeros((seqs, LANES - ROT, length), F32)
    return tuple(
        jnp.concatenate(parts, axis=1).swapaxes(1, 2)
        for parts in (
            (cosine, cosine, rest + 1.0),
            (-sine, none, rest),
            (none, sine, rest),
        )
    )


def spin(values, keep, from_right, from_left):
    low, high = values[:, :LANES], values[:, LANES:]
    half = ROT // 2
    turned = (
        low * keep
        + pltpu.roll(low, LANES - half, 1) * from_right
        + pltpu.roll(low, half, 1) * from_left
    )
    return jnp.concatenate([turned, high], axis=1)


def spin_back(grads, keep, from_right, from_left):
    low, high = grads[:, :LANES], grads[:, LANES:]
    half = ROT // 2
    turned = (
        low * keep
        + pltpu.roll(low * from_right, half, 1)
        + pltpu.roll(low * from_left, LANES - half, 1)
    )
    return jnp.concatenate([turned, high], axis=1)


def block_scores(q, k, seg_col, seg_row, at, upto):
    raw = dot_rt(q, k) * HD ** (-0.5)
    rows = lax.broadcasted_iota(jnp.int32, raw.shape, 0) + at
    columns = lax.broadcasted_iota(jnp.int32, raw.shape, 1)
    allowed = (seg_col[at:upto] == seg_row[:, :upto]) & (rows >= columns)
    return jnp.where(allowed, raw, -1e30)


def row_stats(values):
    center = values - jnp.mean(values, axis=-1, keepdims=True)
    spread = jnp.mean(center * center, axis=-1, keepdims=True)
    inverse = lax.rsqrt(spread + EPS)
    return center * inverse, inverse


def row_blocks(length):
    return [(at, min(at + RB, length)) for at in range(0, length, RB)]


def forward_kernel(heads, count, with_pulled, fresh, *refs):
    (
        lane, rows, gains, shifts, w_qkv, b_qkv, keep, from_right, from_left, seg_col, seg_row,
        w_out, w_fc, b_fc, w_proj, added,
    ) = refs[:16]
    refs = refs[16:]
    if with_pulled:
        pulled, refs = refs[0], refs[1:]
    if not fresh:
        refs = refs[5:]
    n1, n2, o_out, a_out, side_out, q_out, k_out, v_out, lse_out = refs[:9]
    pieces, total = refs[9:-1], refs[-1]
    step = pl.program_id(0)
    length = rows.shape[0]

    @pl.when(step == 0)
    def _():
        for at in range(0, length, LB):
            to = at + LB
            hat, _ = row_stats(rows[at:to, :].astype(F32))
            n1[at:to, :] = (hat * gains[0:1, :] + shifts[0:1, :]).astype(BF)
            n2[at:to, :] = (hat * gains[1:2, :] + shifts[1:2, :]).astype(BF)

    @pl.when(step < heads)
    def _():
        tables = (keep[...], from_right[...], from_left[...])
        mixed = dot(n1[...], w_qkv[...]) + b_qkv[...]
        q_out[...] = spin(mixed[:, :HD], *tables).astype(BF)
        k_out[...] = spin(mixed[:, HD : 2 * HD], *tables).astype(BF)
        v_out[...] = mixed[:, 2 * HD :].astype(BF)
        for at in range(0, length, QB):
            upto = at + QB
            scores = block_scores(
                q_out[at:upto, :], k_out[:upto, :], seg_col, seg_row, at, upto
            )
            peak = jnp.max(scores, axis=-1, keepdims=True)
            raised = jnp.exp(scores - peak)
            weight = jnp.sum(raised, axis=-1, keepdims=True)
            probs = (raised / weight).astype(BF)
            o_out[at:upto, :] = dot(probs, v_out[:upto, :]).astype(BF)
            lse_out[0, at:upto, :] = peak + jnp.log(weight)
        part = dot(o_out[...], w_out[...])

        @pl.when(step == 0)
        def _():
            total[...] = part

        @pl.when(step > 0)
        def _():
            total[...] += part

    @pl.when(step >= heads)
    def _():
        for at, to in row_blocks(length):
            u = dot(n2[at:to, :], w_fc[...]) + b_fc[...]
            half_erf = 0.5 * (1.0 + lax.erf(u * 0.7071067811865476))
            a = (u * half_erf).astype(BF)
            slope = half_erf + u * jnp.exp(-0.5 * u * u) * 0.3989422804014327
            if with_pulled:
                slope = slope * pulled[at:to, :].astype(F32)
            a_out[at:to, :] = a
            side_out[at:to, :] = slope.astype(BF)
            total[at:to, :] += dot(a, w_proj[...])

    @pl.when(step == pl.num_programs(0) - 1)
    def _():
        size = length // count
        for d in range(count):
            at = pl.multiple_of(lax.rem(lane[0] + d, count) * size, size)
            part = total[pl.ds(at, size), :]
            if d == 0:
                part = part + rows[pl.ds(at, size), :].astype(F32) + added[...]
            pieces[d][...] = part.astype(BF)


def fixed(shape, *lead):
    block = (None,) * (len(lead) - 1) + tuple(shape) if len(lead) > 1 else tuple(shape)
    index = tuple(lead) + (0,) * (len(block) - len(lead))
    return pl.BlockSpec(block, lambda i: index)


def forward_pass(rows, s, scalars, tables, seg_col, seg_row, weights, added, pulled, joint):
    gains, shifts, w_qkv, b_qkv, w_out, w_fc, b_fc, w_proj = weights
    rows, at = rows
    _, length, width = rows.shape
    seqs = seg_col.shape[0]
    lane, count = scalars
    heads = w_out.shape[0] // HD
    hidden = w_fc.shape[1]
    tiles = hidden // FT
    head = lambda i: jnp.minimum(i, heads - 1)
    tile = lambda i: jnp.maximum(i - heads, 0)
    by_head = lambda r, c, s=0: pl.BlockSpec((r, c), lambda i: (s, head(i)))
    by_tile = lambda r, c, s=0: pl.BlockSpec((r, c), lambda i: (s, tile(i)))
    shape = jax.ShapeDtypeStruct
    block = length // count
    operands = [
        lane, rows, gains, shifts, w_qkv, b_qkv[None], *tables, seg_col, seg_row, w_out, w_fc,
        b_fc[None], w_proj, added[None],
    ]
    in_specs = [
        pl.BlockSpec(memory_space=pltpu.SMEM),
        fixed((length, width), at, 0),
        fixed((2, width)),
        fixed((2, width)),
        by_head(width, 3 * HD),
        by_head(1, 3 * HD),
        *[fixed((length, LANES), s, 0)] * 3,
        fixed((length, 1), s, 0),
        fixed((1, length), s, 0),
        pl.BlockSpec((HD, width), lambda i: (head(i), 0)),
        by_tile(width, FT),
        by_tile(1, FT),
        pl.BlockSpec((FT, width), lambda i: (tile(i), 0)),
        fixed((1, width)),
    ]
    if pulled is not None:
        operands.append(pulled)
        in_specs.append(by_tile(length, FT, s))
    aliases = {}
    if joint is not None:
        aliases = {len(operands) + i: i for i in range(5)}
        operands += joint
        in_specs += [pl.BlockSpec(memory_space=pl.ANY)] * 5
    flops = 2 * length * width * (4 * heads * HD + 2 * hidden)
    rows_all = seqs * length
    result = pl.pallas_call(
        functools.partial(forward_kernel, heads, count, pulled is not None, joint is None),
        grid=(heads + tiles,),
        in_specs=in_specs,
        out_specs=[
            fixed((length, width), s),
            fixed((length, width), s),
            by_head(length, HD, s),
            by_tile(length, FT, s),
            by_tile(length, FT, s),
            *[by_head(length, HD)] * 3,
            pl.BlockSpec((1, length, 1), lambda i: (head(i), 0, 0)),
            *[fixed((block, width))] * count,
        ],
        out_shape=[
            shape((rows_all, width), BF),
            shape((rows_all, width), BF),
            shape((rows_all, heads * HD), BF),
            shape((rows_all, hidden), BF),
            shape((rows_all, hidden), BF),
            *[shape((length, heads * HD), BF)] * 3,
            shape((heads, length, 1), F32),
            *[shape((block, width), BF)] * count,
        ],
        scratch_shapes=[pltpu.VMEM((length, width), F32)],
        input_output_aliases=aliases,
        cost_estimate=pl.CostEstimate(
            flops=flops, bytes_accessed=2 * width * (4 * heads * HD + 2 * hidden), transcendentals=0
        ),
        compiler_params=pltpu.CompilerParams(vmem_limit_bytes=60 << 20),
    )(*operands)
    return result[:5], ((rows, at), *result[5:9]), result[9:]


def backward_kernel(heads, count, ready, fresh, *refs):
    (
        lane, rows, gains, q, k, v, lse, keep, from_right, from_left, seg_col, seg_row, w_qkv,
        side, w_fc,
    ) = refs[:15]
    refs = refs[15:]
    if ready:
        (d_o, own_dy), refs = refs[:2], refs[2:]
    else:
        (flag, dyb, w_out, w_proj), refs = refs[:4], refs[4:]
        late, refs = refs[:count], refs[count:]
    if not fresh:
        refs = refs[1 if ready else 2 :]
    d_mixed, refs = refs[0], refs[1:]
    if not ready:
        d_u, refs = refs[0], refs[1:]
    sums, d_bqkv, d_bfc = refs[:3]
    pieces = refs[3 : 3 + count]
    one, two, dk_acc, dv_acc = refs[3 + count :]
    step = pl.program_id(0)
    length = rows.shape[0]
    scale = HD ** (-0.5)

    @pl.when(step < heads)
    def _():
        tables = (keep[...], from_right[...], from_left[...])
        total_q = jnp.zeros((1, HD), F32)
        out = d_o[...] if ready else dot_rt(dyb[...], w_out[...]).astype(BF)
        for at in reversed(range(0, length, QB)):
            upto = at + QB
            q_now, d_now = q[at:upto, :], out[at:upto]
            scores = block_scores(q_now, k[:upto, :], seg_col, seg_row, at, upto)
            probs = jnp.exp(scores - lse[0, at:upto, :])
            d_probs = dot_rt(d_now, v[:upto, :])
            row = jnp.sum(probs * d_probs, axis=-1, keepdims=True)
            d_scores = (probs * (d_probs - row)).astype(BF)
            dq = dot(d_scores, k[:upto, :]) * scale
            dq = spin_back(dq, *(t[at:upto] for t in tables)).astype(BF)
            d_mixed[at:upto, :HD] = dq
            total_q += jnp.sum(dq.astype(F32), axis=0, keepdims=True)
            if upto == length:
                dk_acc[...] = dot_lt(d_scores, q_now)
                dv_acc[...] = dot_lt(probs.astype(BF), d_now)
            else:
                dk_acc[:upto, :] += dot_lt(d_scores, q_now)
                dv_acc[:upto, :] += dot_lt(probs.astype(BF), d_now)
        dk = spin_back(dk_acc[...] * scale, *tables).astype(BF)
        d_mixed[:, HD : 2 * HD] = dk
        dv = dv_acc[...].astype(BF)
        d_mixed[:, 2 * HD :] = dv
        d_bqkv[:, :HD] = total_q
        d_bqkv[:, HD : 2 * HD] = jnp.sum(dk.astype(F32), axis=0, keepdims=True)
        d_bqkv[:, 2 * HD :] = jnp.sum(dv.astype(F32), axis=0, keepdims=True)
        part = dot_rt(d_mixed[...], w_qkv[...])

        @pl.when(step == 0)
        def _():
            one[...] = part

        @pl.when(step > 0)
        def _():
            one[...] += part

    def tile_step(start):
        bias = jnp.zeros(d_bfc.shape, F32)
        for at, to in row_blocks(length):
            if ready:
                d_now = side[at:to, :]
            else:
                d_now = dot_rt(dyb[at:to, :], w_proj[...]) * side[at:to, :].astype(F32)
                d_now = d_now.astype(BF)
                d_u[at:to, :] = d_now
            bias += jnp.sum(d_now.astype(F32), axis=0, keepdims=True)
            part = dot_rt(d_now, w_fc[...])
            if start:
                two[at:to, :] = part
            else:
                two[at:to, :] += part
        d_bfc[...] = bias

    pl.when(step == heads)(lambda: tile_step(True))
    pl.when(step > heads)(lambda: tile_step(False))

    @pl.when(step == pl.num_programs(0) - 1)
    def _():
        found = [jnp.zeros((1, rows.shape[1]), F32) for _ in range(4)]
        size = length // count
        for d in range(count):
            at = pl.multiple_of(lax.rem(lane[0] + d, count) * size, size)
            now = pl.ds(at, size)
            hat, inverse = row_stats(rows[now, :].astype(F32))
            first, second = one[now, :], two[now, :]
            for i, term in enumerate((first * hat, second * hat, first, second)):
                found[i] += jnp.sum(term, axis=0, keepdims=True)
            both = first * gains[0:1, :] + second * gains[1:2, :]
            both = (
                both
                - jnp.mean(both, axis=-1, keepdims=True)
                - hat * jnp.mean(both * hat, axis=-1, keepdims=True)
            ) * inverse
            if d == 0:
                both = both + (own_dy[...] if ready else dyb[now, :]).astype(F32)
            both = both.astype(BF)
            if not ready:
                both = jnp.where(flag[0] == 0, both, late[d][...])
            pieces[d][...] = both
        for i in range(4):
            sums[i : i + 1, :] = found[i]


def backward_pass(kept, side, s, scalars, tables, seg_col, seg_row, weights, ready, late, joint):
    gains, _, w_qkv, _, w_out, w_fc, _, w_proj = weights
    (rows, row_at), q, k, v, lse = kept
    _, length, width = rows.shape
    lane, count = scalars
    seqs = seg_col.shape[0]
    heads = w_out.shape[0] // HD
    hidden = w_fc.shape[1]
    tiles = hidden // FT
    head = lambda i: jnp.minimum(i, heads - 1)
    tile = lambda i: jnp.maximum(i - heads, 0)
    by_head = lambda r, c, s=0: pl.BlockSpec((r, c), lambda i: (s, head(i)))
    by_tile = lambda r, c, s=0: pl.BlockSpec((r, c), lambda i: (s, tile(i)))
    shape = jax.ShapeDtypeStruct
    block = length // count
    smem = pl.BlockSpec(memory_space=pltpu.SMEM)
    operands = [lane, rows, gains, q, k, v, lse, *tables, seg_col, seg_row, w_qkv, side, w_fc]
    in_specs = [
        smem,
        fixed((length, width), row_at, 0),
        fixed((2, width)),
        *[by_head(length, HD)] * 3,
        pl.BlockSpec((1, length, 1), lambda i: (head(i), 0, 0)),
        *[fixed((length, LANES), s, 0)] * 3,
        fixed((length, 1), s, 0),
        fixed((1, length), s, 0),
        by_head(width, 3 * HD),
        by_tile(length, FT, s),
        by_tile(width, FT),
    ]
    rows_all = seqs * length
    out_specs = [by_head(length, 3 * HD, s)]
    out_shape = [shape((rows_all, 3 * heads * HD), BF)]
    if ready is not None:
        operands += list(ready)
        in_specs += [by_head(length, HD, s), fixed((block, width))]
    else:
        flag, dyb, others = late
        operands += [flag, dyb, w_out, w_proj, *others]
        in_specs += [
            smem,
            fixed((length, width)),
            pl.BlockSpec((HD, width), lambda i: (head(i), 0)),
            pl.BlockSpec((FT, width), lambda i: (tile(i), 0)),
            *[fixed((block, width))] * count,
        ]
        out_specs.append(by_tile(length, FT, s))
        out_shape.append(shape((rows_all, hidden), BF))
    aliases = {}
    if joint is not None:
        aliases = {len(operands) + i: i for i in range(len(joint))}
        operands += joint
        in_specs += [pl.BlockSpec(memory_space=pl.ANY)] * len(joint)
    n_joint = len(out_specs)
    out_specs += [fixed((4, width)), by_head(1, 3 * HD), by_tile(1, FT)]
    out_specs += [fixed((block, width))] * count
    out_shape += [
        shape((4, width), F32),
        shape((1, 3 * heads * HD), F32),
        shape((1, hidden), F32),
        *[shape((block, width), BF)] * count,
    ]
    flops = 2 * length * width * (3 * heads * HD + hidden) * (1 if ready is not None else 2)
    result = pl.pallas_call(
        functools.partial(backward_kernel, heads, count, ready is not None, joint is None),
        grid=(heads + tiles,),
        in_specs=in_specs,
        out_specs=out_specs,
        out_shape=out_shape,
        scratch_shapes=[pltpu.VMEM((length, width), F32)] * 2
        + [pltpu.VMEM((length, HD), F32)] * 2,
        input_output_aliases=aliases,
        cost_estimate=pl.CostEstimate(
            flops=flops, bytes_accessed=2 * width * (3 * heads * HD + hidden), transcendentals=0
        ),
        compiler_params=pltpu.CompilerParams(vmem_limit_bytes=60 << 20),
    )(*operands)
    joint, rest = result[:n_joint], result[n_joint:]
    sums, d_bqkv, d_bfc = rest[:3]
    return joint, (sums, d_bqkv[0], d_bfc[0]), rest[3:]


def tie(values, *earlier):
    return lax.optimization_barrier((values, earlier))[0]


def shards(
    boundary_in,
    segment_ids,
    norm_gains,
    norm_biases,
    w_qkv,
    b_qkv,
    w_out,
    w_fc,
    b_fc,
    w_proj,
    out_biases,
):
    w_qkv, w_out, w_fc, w_proj = w_qkv[0], w_out[0], w_fc[0], w_proj[0]
    b_qkv, b_fc = b_qkv[0].astype(F32), b_fc[0].astype(F32)
    gains, shifts = norm_gains[0].astype(F32), norm_biases[0].astype(F32)
    added = out_biases[0, 0].astype(F32) + out_biases[0, 1].astype(F32)
    weights = (gains, shifts, w_qkv, b_qkv, w_out, w_fc, b_fc, w_proj)
    seqs, length = segment_ids.shape
    flat = boundary_in[0]
    ends = flat.reshape(seqs, length, -1)
    section = lax.axis_index("section")
    lane = lax.axis_index("tensor")
    count = lax.axis_size("tensor")
    first = section == 0
    dp = lax.axis_index("dp")
    dp_count = lax.axis_size("dp")
    scalars = (lane[None], count)
    tables = rotary_tables(segment_ids)
    columns, lines = segment_ids[:, :, None], segment_ids[:, None, :]

    def own(values, at=0):
        size = length // count
        return lax.dynamic_slice_in_dim(values, at * length + lane * size, size, 0)

    def ring(step, origin, target):
        return [(origin * count + i, target * count + (i + step) % count) for i in range(count)]

    both = ("section", "tensor")

    def scatter(blocks, origin):
        pieces = []
        for step, block in enumerate(blocks):
            pieces.append(lax.ppermute(block, both, ring(step, origin, 1 - origin)))
        return pieces

    def scatter_within(blocks):
        pieces = [blocks[0]]
        for step in range(1, count):
            route = [(i, (i + step) % count) for i in range(count)]
            pieces.append(lax.ppermute(blocks[step], "tensor", route))
        return pieces

    def summed(pieces):
        return functools.reduce(jnp.add, [p.astype(F32) for p in pieces]).astype(BF)

    def gather(block, where=None):
        size = block.shape[0]
        whole = jnp.zeros((count * size,) + block.shape[1:], block.dtype)
        for step in range(count):
            piece = block
            if step:
                if where is None:
                    route = [(i, (i + step) % count) for i in range(count)]
                    piece = lax.ppermute(block, "tensor", route)
                else:
                    piece = lax.ppermute(block, both, ring(step, where, where))
            whole = lax.dynamic_update_slice_in_dim(
                whole, piece, ((lane - step) % count) * size, 0
            )
        return whole

    def forward(rows, s, joint, pulled=None):
        return forward_pass(rows, s, scalars, tables, columns, lines, weights, added, pulled, joint)

    def backward(kept, side, s, joint, ready=None, late=None):
        return backward_pass(
            kept, side, s, scalars, tables, columns, lines, weights, ready, late, joint
        )

    early, pieces, joint, before = [], [], None, None
    for s in range(seqs):
        rows = ends if s == 0 else tie(ends, before)
        joint, kept, before = forward((rows, s), s, joint)
        early.append(((ends, s), *kept[1:]))
        pieces.append(scatter(before, 0))
    joint_early = joint
    blocks = []
    for s in range(seqs):
        if s == 1:
            pulled = dot_rt(tie(flat, blocks[0]), w_proj).astype(BF)
            d_o = dot_rt(tie(flat, pulled), w_out).astype(BF)
            before = (pulled, d_o)
        pieces[s][0] = tie(pieces[s][0], before, *blocks)
        blocks.append(summed(pieces[s]))
    inputs = [gather(block, 1) for block in blocks]
    inputs[0] = tie(inputs[0], blocks[-1])

    late_out, small_late, pieces = [], [], []
    joint, joint_back, before = None, None, None
    for s in range(seqs):
        rows = inputs[s] if s == 0 else tie(inputs[s], before)
        joint, kept, out = forward((rows[None], 0), s, joint, pulled)
        late_out.append(out)
        ready = (d_o, own(flat, s))
        joint_back, small, before = backward(kept, joint[4], s, joint_back, ready)
        small_late.append(small)
        pieces.append(scatter(before, 1))
    n1, n2, o, a, d_u = joint
    (d_mixed,) = joint_back
    pieces[0][0] = tie(pieces[0][0], before)
    blocks = [summed(pieces[0])]
    pairs = [(a, flat), (o, flat), (n2, d_u), (n1, d_mixed)]
    whole_late, before = [], blocks[0]
    for w, (left, right) in enumerate(pairs):
        if w == 3:
            for s in range(1, seqs):
                pieces[s][0] = tie(pieces[s][0], before, *blocks)
                blocks.append(summed(pieces[s]))
            before = blocks[-1]
        before = dot_lt(tie(left, before), right).astype(BF)
        whole_late.append(before)
    returning = [gather(block, 0) for block in blocks]

    half_dp = dp_count // 2
    group, core = dp // 2, dp % 2
    away = [((group + g) % half_dp) * 2 + 1 - core for g in range(half_dp)]
    near = [((group + g) % half_dp) * 2 + core for g in range(half_dp)]
    n1, n2, o, a, slope = joint_early
    arrived, others, mine = {}, {}, {}

    def part_of(w, block, left, right, before):
        cut_left = w >= 2
        cut = left if cut_left else right
        size = cut.shape[1] // dp_count
        left, right = tie((left, right), before)
        cut = lax.dynamic_slice_in_dim(left if cut_left else right, block * size, size, 1)
        early = dot_lt(cut, right) if cut_left else dot_lt(left, cut)
        kept = lax.dynamic_slice_in_dim(
            whole_late[w], block * size, size, 0 if cut_left else 1
        )
        return jnp.where(first, early, kept.astype(F32))

    def leave(pairs, groups, before):
        for w, left, right in pairs:
            for g in groups:
                before = part_of(w, away[g], left, right, before).astype(BF)
                arrived[w, g] = lax.ppermute(before, "dp", [(i, i ^ 1) for i in range(dp_count)])
        return before

    def pass_on(pairs, before):
        for w, left, right in pairs:
            for g in range(1, half_dp):
                part = part_of(w, near[g], left, right, before)
                before = (part + arrived[w, g].astype(F32)).astype(BF)
                route = [(i, (i + 2 * g) % dp_count) for i in range(dp_count)]
                others.setdefault(w, []).append(lax.ppermute(before, "dp", route))
        return before

    small_early, pieces, joint_back = [], [], None
    for s in range(seqs):
        dyb = tie(returning[s], before)
        if s == seqs - 1:
            dy_all = jnp.concatenate(returning[:-1] + [dyb], 0)
            ends_pairs = [(0, a, dy_all), (1, o, dy_all)]
            before = leave(ends_pairs, range(1, half_dp), before)
            before = pass_on(ends_pairs, before)
            dyb = tie(dyb, before)
        flag = section[None]
        joint_back, small, before = backward(
            early[s], slope, s, joint_back, late=(flag, dyb, late_out[s])
        )
        small_early.append(small)
        pieces.append(scatter_within(before))
    d_mixed, d_u = joint_back
    inner_pairs = [(2, n2, d_u), (3, n1, d_mixed)]

    results, blocks = [], []
    for s in range(seqs - 1):
        pieces[s][0] = tie(pieces[s][0], before)
        blocks.append(summed(pieces[s]))
    before = (before, blocks)
    before = leave(inner_pairs, range(1, half_dp), before)
    before = pass_on(inner_pairs, before)
    small = [
        jnp.where(first, functools.reduce(jnp.add, x), functools.reduce(jnp.add, y))
        for x, y in zip(zip(*small_early), zip(*small_late))
    ]
    d_norm, d_bqkv, d_bfc = small
    d_outb = jnp.sum(jnp.where(first, dy_all, flat).astype(F32), axis=0)
    packed = [
        x.reshape(x.shape[0] * parts, dp_count, -1).swapaxes(0, 1).reshape(dp_count, -1)
        for x, parts in ((d_norm, count), (d_bqkv[None], 1), (d_bfc[None], 1), (d_outb[None], 1))
    ]
    sizes = [x.shape[1] for x in packed]
    packed = jnp.concatenate(packed, axis=1)
    packed = tie(packed, before)
    parts = [lax.dynamic_index_in_dim(packed, dp, 0, keepdims=True)]
    for step in range(1, dp_count):
        block = lax.dynamic_index_in_dim(packed, (dp + step) % dp_count, 0, keepdims=True)
        route = [(i, (i + step) % dp_count) for i in range(dp_count)]
        parts.append(lax.ppermute(block, "dp", route))
    pieces[-1][0] = tie(pieces[-1][0], before)
    blocks.append(summed(pieces[-1]))
    results = [gather(block) for block in blocks]
    pairs = ends_pairs + inner_pairs
    before = leave(pairs, [0], (before, blocks))
    for w, left, right in pairs:
        before = part_of(w, near[0], left, right, before)
        mine[w] = before + arrived[w, 0].astype(F32)
    parts[0] = tie(parts[0], mine)
    total = functools.reduce(jnp.add, parts)
    edges = [sum(sizes[:i]) for i in range(len(sizes) + 1)]
    norm, g_bqkv, g_bfc, g_outb = [total[0, edges[i] : edges[i + 1]] for i in range(len(sizes))]
    norm = norm.reshape(4, count, -1).swapaxes(0, 1)
    g_norm = lax.dynamic_index_in_dim(norm, lane, 0, keepdims=False)
    for step in range(1, count):
        block = lax.dynamic_index_in_dim(norm, (lane + step) % count, 0, keepdims=False)
        route = [(i, (i + step) % count) for i in range(count)]
        g_norm = g_norm + lax.ppermute(block, "tensor", route)

    g_proj, g_out, g_fc, g_qkv = [
        functools.reduce(jnp.add, [x.astype(F32) for x in others[w]], mine[w]) for w in range(4)
    ]
    boundary_out = jnp.concatenate(results, 0).astype(F32)[None]
    return (
        boundary_out,
        g_norm[None, :2],
        g_norm[None, 2:],
        g_qkv[None],
        g_bqkv[None],
        g_out[None],
        g_fc[None],
        g_bfc[None],
        g_proj[None],
        jnp.stack([g_outb, g_outb])[None],
    )


def solution(mesh):
    step = build(mesh)
    return step


def build(mesh):
    return jax.shard_map(
        shards,
        mesh=mesh,
        in_specs=(
            P("section", "dp", None),
            P("dp", None),
            P("section", None, None),
            P("section", None, None),
            P("section", None, "tensor"),
            P("section", "tensor"),
            P("section", "tensor", None),
            P("section", None, "tensor"),
            P("section", "tensor"),
            P("section", "tensor", None),
            P("section", None, None),
        ),
        out_specs=(
            P("section", "dp", None),
            P("section", None, ("tensor", "dp")),
            P("section", None, ("tensor", "dp")),
            P("section", "dp", "tensor"),
            P("section", ("tensor", "dp")),
            P("section", "tensor", "dp"),
            P("section", "dp", "tensor"),
            P("section", ("tensor", "dp")),
            P("section", "tensor", "dp"),
            P("section", None, "dp"),
        ),
        check_vma=False,
    )
```

time: 899 us -> 786 us (0.87)
  Pallas kernels: 279 us -> 235 us
  local copies, waits for them, and re-layouts: 70.2 us -> 27.1 us
  other arithmetic: 71.5 us -> 44.9 us
  starting transfers between devices: 197 us -> 176 us
  waiting for transfers between devices: 144 us -> 164 us
    pallas_call x8, Pallas kernels: 279 us -> 235 us  [the longest x4 121 us: forward_pass(): pl.pallas_call(functools.partial(forward_kernel, heads, count, pulled is...]
    unnamed x224 -> x84, local copies, waits for them, and re-layouts: 35.1 us -> 4.19 us
    ppermute x20 -> x24, waiting for transfers between devices: 30.1 us -> 59.1 us  [the longest x4 56.6 us: pass_on(): others.setdefault(w, []).append(lax.ppermute(before, 'dp', route))]
    ppermute x20 -> x24, starting transfers between devices: 83.4 us -> 70.7 us  [the longest x6 39.1 us: scatter_within(): pieces.append(lax.ppermute(blocks[step], 'tensor', route))]
    ppermute x6, starting transfers between devices: 27.1 us -> 16.2 us  [gather(): piece = lax.ppermute(block, 'tensor', route)]
    another operation x8 -> x0, other arithmetic: 10.5 us -> none  [the longest x4 9.85 us: shards(): jnp.stack([chosen(w, b, grads_late[w, 'away', g]).astype(BF) for g, b in...]
    dot_general x36 -> x22, matrix products: 125 us -> 127 us  [dot_f32(): lax.dot_general(left, right, (dims, ((), ())), preferred_element_type=F32)]
  transfers between devices with their start and end apart: 54 -> 58, of which waited for: 13 -> 18; matrix products, arithmetic and copies ran while one was open for 20% -> 22% of each run, Pallas kernels for 23% -> 26%
where the time goes in v1:
time: 786 us; the launch traced here: 776 us
  Pallas kernels  235 us (30%)
  starting transfers between devices  176 us (22%)
  waiting for transfers between devices  164 us (21%)
  matrix products  127 us (16%)
  other arithmetic  44.9 us (6%)
  local copies, waits for them, and re-layouts  27.1 us (3%)
    dot_general x22, matrix products, dot_f32(): lax.dot_general(left, right, (dims, ((), ())), preferred_element_type=F32)  127 us
    pallas_call x4, Pallas kernels, forward_pass(): pl.pallas_call(functools.partial(forward_kernel, heads, count, pulled is...  121 us
    pallas_call x4, Pallas kernels, backward_pass(): pl.pallas_call(functools.partial(backward_kernel, heads, count, ready is...  114 us
    ppermute x4, waiting for transfers between devices, pass_on(): others.setdefault(w, []).append(lax.ppermute(before, 'dp', route))  56.6 us
    ppermute x12, starting transfers between devices, gather(): piece = lax.ppermute(block, both, ring(step, where, where))  56 us
    ppermute x6, waiting for transfers between devices, gather(): piece = lax.ppermute(block, 'tensor', route)  55 us
    ppermute x6, starting transfers between devices, scatter_within(): pieces.append(lax.ppermute(blocks[step], 'tensor', route))  39.1 us
    ppermute x16, waiting for transfers between devices, scatter(): pieces.append(lax.ppermute(block, both, ring(step, origin, 1 - origin)))  38.9 us
  transfers between devices with their start and end apart: 58, of which 18 were waited for; matrix products, arithmetic and copies ran while one was open for 22% of the time, Pallas kernels for 26%

profile of v1, /device:TPU:0, one launch (start us, length us, event | category | flops | bytes accessed | tf_op | source)
XLA Modules:
  0.0 776.1 jit_solution(17960497774396338154)
XLA Ops:
  14.0 29.8 %shard_map.186 = (bf16[1024,2048]{1,0:T(8,128)(2,1)}, bf16[1024,2048]{1,0:T(8,128)(2,1)}, bf16[1024,512]{1,0:T(8,128)(2,1)}, bf16[1024,2048]{1,0:T(8,128)(2,1)},...) custom-call(s32[1]{0:T(128)} %bitcast.refs_0_, ...), custom_call_target="tpu_custom_call" | custom-call | flops 12884901888 | bytes 25165824 | tf_op jit(solution)/shard_map/pallas_call | solution.py:226
  55.9 30.0 %shard_map.187 = (bf16[1024,2048]{1,0:T(8,128)(2,1)}, bf16[1024,2048]{1,0:T(8,128)(2,1)}, bf16[1024,512]{1,0:T(8,128)(2,1)}, bf16[1024,2048]{1,0:T(8,128)(2,1)},...) custom-call(s32[1]{0:T(128)} %bitcast.refs_0_, ...), custom_call_target="tpu_custom_call", output_to_operand_aliasing={{0}: (16, {}), {1}: (17, {}), {2}: (18, {}), {3}: (19, {}),... | custom-call | flops 12884901888 | bytes 25165824 | tf_op jit(solution)/shard_map/pallas_call | solution.py:226
  107.9 12.7 %convolution_convert_fusion.3.refs_16_ = bf16[1024,2048]{1,0:T(8,128)(2,1)} fusion(bf16[1024,2048]{1,0:T(8,128)(2,1)S(1)} %bitcast.126, bf16[1,2048,2048]{2,1,0:T(8,128)(2,1)} %param.20), kind=kOutput, calls=%fused_computation.18 | convolution fusion | flops 8592031744 | bytes 16777216 | tf_op jit(solution)/shard_map/dot_general | solution.py:23
  137.4 30.3 %shard_map.188 = (bf16[1024,2048]{1,0:T(8,128)(2,1)}, bf16[1024,2048]{1,0:T(8,128)(2,1)}, bf16[1024,512]{1,0:T(8,128)(2,1)}, bf16[1024,2048]{1,0:T(8,128)(2,1)},...) custom-call(s32[1]{0:T(128)} %bitcast.refs_0_, ...), custom_call_target="tpu_custom_call" | custom-call | flops 12884901888 | bytes 25165824 | tf_op jit(solution)/shard_map/pallas_call | solution.py:226
  167.8 23.8 %shard_map.189 = (bf16[1024,1536]{1,0:T(8,128)(2,1)}, f32[4,2048]{1,0:T(4,128)}, f32[1,1536]{1,0:T(1,128)}, f32[1,2048]{1,0:T(1,128)}, bf16[128,2048]{1,0:T(8,12...) custom-call(s32[1]{0:T(128)} %bitcast.refs_0_, ...), custom_call_target="tpu_custom_call" | custom-call | flops 7516192768 | bytes 14680064 | tf_op jit(solution)/shard_map/pallas_call | solution.py:433
  198.3 30.8 %shard_map.190 = (bf16[1024,2048]{1,0:T(8,128)(2,1)}, bf16[1024,2048]{1,0:T(8,128)(2,1)}, bf16[1024,512]{1,0:T(8,128)(2,1)}, bf16[1024,2048]{1,0:T(8,128)(2,1)},...) custom-call(s32[1]{0:T(128)} %bitcast.refs_0_, ...), custom_call_target="tpu_custom_call", output_to_operand_aliasing={{0}: (17, {}), {1}: (18, {}), {2}: (19, {}), {3}: (20, {}),... | custom-call | flops 12884901888 | bytes 25165824 | tf_op jit(solution)/shard_map/pallas_call | solution.py:226
  229.1 23.7 %shard_map.191 = (bf16[1024,1536]{1,0:T(8,128)(2,1)}, f32[4,2048]{1,0:T(4,128)}, f32[1,1536]{1,0:T(1,128)}, f32[1,2048]{1,0:T(1,128)}, bf16[128,2048]{1,0:T(8,12...) custom-call(s32[1]{0:T(128)} %bitcast.refs_0_, ...), custom_call_target="tpu_custom_call", output_to_operand_aliasing={{0}: (17, {})} | custom-call | flops 7516192768 | bytes 14680064 | tf_op jit(solution)/shard_map/pallas_call | solution.py:433
  257.9 20.5 %collective-permute-done.16 = bf16[128,2048]{1,0:T(8,128)(2,1)} collective-permute-done((bf16[128,2048]{1,0:T(8,128)(2,1)}, bf16[128,2048]{1,0:T(8,128)(2,1)}, u32[]{:S(2)}, u32[]{:S(2)}) %collective-permute-start.16) | collective-permute-done | bytes 524320 | tf_op jit(solution)/shard_map/ppermute | solution.py:499
  294.0 13.9 %convolution_convert_fusion.2 = bf16[2048,2048]{1,0:T(8,128)(2,1)} fusion(bf16[1024,2048]{1,0:T(8,128)(2,1)} %get-tuple-element.201, bf16[1,1024,2048]{2,1,0:T(8,128)(2,1)S(1)} %copy-done.2), kind=kOutput, calls=%fused_computation.3 | convolution fusion | flops 8594128896 | bytes 16777216 | tf_op jit(solution)/shard_map/dot_general | solution.py:23
  311.7 11.4 %convolution_convert_fusion.1 = bf16[2048,2048]{1,0:T(8,128)(2,1)} fusion(bf16[1024,2048]{1,0:T(8,128)(2,1)S(1)} %copy-done.16, bf16[1024,2048]{1,0:T(8,128)(2,1)S(1)} %copy-done.9), kind=kOutput, calls=%fused_computation.2 | convolution fusion | flops 8594128896 | bytes 16777216 | tf_op jit(solution)/shard_map/dot_general | solution.py:23
  323.1 33.4 %collective-permute-start.19 = (bf16[128,2048]{1,0:T(8,128)(2,1)S(1)}, bf16[128,2048]{1,0:T(8,128)(2,1)S(1)}, u32[]{:S(2)}, u32[]{:S(2)}) collective-permute-start(bf16[128,2048]{1,0:T(8,128)(2,1)S(1)} %get-tuple-element.297), channel_id=1, source_target_pairs={{0,8},{4,12},{8,0},{12,4},{1,9},{5,13},{9,1},{13,5},{2,10},{6,14},... | collective-permute-start | bytes 1572872 | tf_op jit(solution)/shard_map/ppermute | solution.py:522
  367.3 8.8 %convolution_convert_fusion = bf16[2048,1536]{1,0:T(8,128)(2,1)} fusion(bf16[1024,2048]{1,0:T(8,128)(2,1)S(1)} %copy-done.15, bf16[1024,1536]{1,0:T(8,128)(2,1)S(1)} %copy-done.21), kind=kOutput, calls=%fused_computation.1 | convolution fusion | flops 6445596672 | bytes 13631488 | tf_op jit(solution)/shard_map/dot_general | solution.py:23
  380.4 8.9 %collective-permute-done.19 = bf16[128,2048]{1,0:T(8,128)(2,1)S(1)} collective-permute-done((bf16[128,2048]{1,0:T(8,128)(2,1)S(1)}, bf16[128,2048]{1,0:T(8,128)(2,1)S(1)}, u32[]{:S(2)}, u32[]{:S(2)}) %collective-permute-start.19) | collective-permute-done | bytes 524320 | tf_op jit(solution)/shard_map/ppermute | solution.py:522
  393.2 33.0 %shard_map.192 = (bf16[1024,1536]{1,0:T(8,128)(2,1)}, bf16[1024,2048]{1,0:T(8,128)(2,1)}, f32[4,2048]{1,0:T(4,128)}, f32[1,1536]{1,0:T(1,128)}, f32[1,2048]{1,0:...) custom-call(s32[1]{0:T(128)} %bitcast.refs_0_, ...), custom_call_target="tpu_custom_call" | custom-call | flops 15032385536 | bytes 14680064 | tf_op jit(solution)/shard_map/pallas_call | solution.py:433
  442.7 12.3 %collective-permute-start.30 = (bf16[128,2048]{1,0:T(8,128)(2,1)}, bf16[128,2048]{1,0:T(8,128)(2,1)}, u32[]{:S(2)}, u32[]{:S(2)}) collective-permute-start(bf16[128,2048]{1,0:T(8,128)(2,1)} %get-tuple-element.217), channel_id=1, source_target_pairs={{0,4},{4,8},{8,12},{12,0},{1,5},{5,9},{9,13},{13,1},{2,6},{6,10},{... | collective-permute-start | bytes 1572872 | tf_op jit(solution)/shard_map/ppermute | solution.py:506
  471.0 33.4 %shard_map.193 = (bf16[1024,1536]{1,0:T(8,128)(2,1)}, bf16[1024,2048]{1,0:T(8,128)(2,1)}, f32[4,2048]{1,0:T(4,128)}, f32[1,1536]{1,0:T(1,128)}, f32[1,2048]{1,0:...) custom-call(s32[1]{0:T(128)} %bitcast.refs_0_, ...), custom_call_target="tpu_custom_call", output_to_operand_aliasing={{0}: (23, {}), {1}: (24, {})} | custom-call | flops 15032385536 | bytes 14680064 | tf_op jit(solution)/shard_map/pallas_call | solution.py:433
  526.2 9.5 %collective-permute-done.33 = bf16[128,2048]{1,0:T(8,128)(2,1)} collective-permute-done((bf16[128,2048]{1,0:T(8,128)(2,1)}, bf16[128,2048]{1,0:T(8,128)(2,1)}, u32[]{:S(2)}, u32[]{:S(2)}) %collective-permute-start.33) | collective-permute-done | bytes 524320 | tf_op jit(solution)/shard_map/ppermute | solution.py:520
  537.7 19.9 %collective-permute-done.34 = bf16[128,2048]{1,0:T(8,128)(2,1)} collective-permute-done((bf16[128,2048]{1,0:T(8,128)(2,1)}, bf16[128,2048]{1,0:T(8,128)(2,1)}, u32[]{:S(2)}, u32[]{:S(2)}) %collective-permute-start.34) | collective-permute-done | bytes 524320 | tf_op jit(solution)/shard_map/ppermute | solution.py:520
  563.1 19.3 %collective-permute-start.40 = (bf16[128,2048]{1,0:T(8,128)(2,1)}, bf16[128,2048]{1,0:T(8,128)(2,1)S(1)}, u32[]{:S(2)}, u32[]{:S(2)}) collective-permute-start(bf16[128,2048]{1,0:T(8,128)(2,1)} %get-tuple-element.241), channel_id=1, source_target_pairs={{0,12},{4,0},{8,4},{12,8},{1,13},{5,1},{9,5},{13,9},{2,14},{6,2},{... | collective-permute-start | bytes 1572872 | tf_op jit(solution)/shard_map/ppermute | solution.py:506
  642.2 19.9 %collective-permute-done.42 = bf16[128,2048]{1,0:T(8,128)(2,1)S(1)} collective-permute-done((bf16[128,2048]{1,0:T(8,128)(2,1)}, bf16[128,2048]{1,0:T(8,128)(2,1)S(1)}, u32[]{:S(2)}, u32[]{:S(2)}) %collective-permute-start.42) | collective-permute-done | bytes 524320 | tf_op jit(solution)/shard_map/ppermute | solution.py:520
  680.9 30.1 %collective-permute-done.56 = bf16[512,2048]{1,0:T(8,128)(2,1)} collective-permute-done((bf16[512,2048]{1,0:T(8,128)(2,1)}, bf16[512,2048]{1,0:T(8,128)(2,1)}, u32[]{:S(2)}, u32[]{:S(2)}) %collective-permute-start.56) | collective-permute-done | bytes 2097184 | tf_op jit(solution)/shard_map/ppermute | solution.py:612
  711.0 12.7 %collective-permute-start.50 = (f32[1,3456]{1,0:T(1,128)S(1)}, f32[1,3456]{1,0:T(1,128)S(1)}, u32[]{:S(2)}, u32[]{:S(2)}) collective-permute-start(f32[1,3456]{1,0:T(1,128)S(1)} %get-tuple-element.309), channel_id=1, source_target_pairs={{0,3},{1,0},{2,1},{3,2},{4,7},{5,4},{6,5},{7,6},{8,11},{9,8},{10,9... | collective-permute-start | bytes 41480 | tf_op jit(solution)/shard_map/ppermute | solution.py:657
  729.2 26.5 %collective-permute-done.57 = bf16[2048,512]{1,0:T(8,128)(2,1)S(1)} collective-permute-done((bf16[2048,512]{1,0:T(8,128)(2,1)}, bf16[2048,512]{1,0:T(8,128)(2,1)S(1)}, u32[]{:S(2)}, u32[]{:S(2)}) %collective-permute-start.57) | collective-permute-done | bytes 2097184 | tf_op jit(solution)/shard_map/ppermute | solution.py:612
  759.2 9.0 %collective-permute-start.51 = (f32[4,128]{1,0:T(4,128)S(1)}, f32[4,128]{1,0:T(4,128)S(1)}, u32[]{:S(2)}, u32[]{:S(2)}) collective-permute-start(f32[4,128]{1,0:T(4,128)S(1)} %bitcast.144), channel_id=1, source_target_pairs={{0,4},{4,8},{8,12},{12,0},{1,5},{5,9},{9,13},{13,1},{2,6},{6,10},{... | collective-permute-start | bytes 6152 | tf_op jit(solution)/shard_map/ppermute | solution.py:675
  (278 shorter events, 270.0 us)
Async XLA Ops:
  132.6 61.5 %collective-permute-start.12 = (bf16[128,2048]{1,0:T(8,128)(2,1)}, bf16[128,2048]{1,0:T(8,128)(2,1)S(1)}, u32[]{:S(2)}, u32[]{:S(2)}) collective-permute-start(bf16[128,2048]{1,0:T(8,128)(2,1)} %get-tuple-element.303), channel_id=1, source_target_pairs={{16,20},{20,24},{24,28},{28,16},{17,21},{21,25},{25,29},{29,17},{1... | collective-permute-start | bytes 1572872 | tf_op jit(solution)/shard_map/ppermute | solution.py:522
  133.3 62.2 %collective-permute-start.13 = (bf16[128,2048]{1,0:T(8,128)(2,1)}, bf16[128,2048]{1,0:T(8,128)(2,1)S(1)}, u32[]{:S(2)}, u32[]{:S(2)}) collective-permute-start(bf16[128,2048]{1,0:T(8,128)(2,1)} %get-tuple-element.303), channel_id=1, source_target_pairs={{16,24},{20,28},{24,16},{28,20},{17,25},{21,29},{25,17},{29,21},{1... | collective-permute-start | bytes 1572872 | tf_op jit(solution)/shard_map/ppermute | solution.py:522
  134.0 62.9 %collective-permute-start.14 = (bf16[128,2048]{1,0:T(8,128)(2,1)}, bf16[128,2048]{1,0:T(8,128)(2,1)S(1)}, u32[]{:S(2)}, u32[]{:S(2)}) collective-permute-start(bf16[128,2048]{1,0:T(8,128)(2,1)} %get-tuple-element.303), channel_id=1, source_target_pairs={{16,28},{20,16},{24,20},{28,24},{17,29},{21,17},{25,21},{29,25},{1... | collective-permute-start | bytes 1572872 | tf_op jit(solution)/shard_map/ppermute | solution.py:522
  191.5 62.8 %collective-permute-start.11 = (bf16[128,2048]{1,0:T(8,128)(2,1)}, bf16[128,2048]{1,0:T(8,128)(2,1)}, u32[]{:S(2)}, u32[]{:S(2)}) collective-permute-start(bf16[128,2048]{1,0:T(8,128)(2,1)} %get-tuple-element.177), channel_id=1, source_target_pairs={{16,0},{20,4},{24,8},{28,12},{17,1},{21,5},{25,9},{29,13},{18,2},{... | collective-permute-start | bytes 1572872 | tf_op jit(solution)/shard_map/ppermute | solution.py:499
  192.8 63.8 %collective-permute-start.15 = (bf16[128,2048]{1,0:T(8,128)(2,1)}, bf16[128,2048]{1,0:T(8,128)(2,1)}, u32[]{:S(2)}, u32[]{:S(2)}) collective-permute-start(bf16[128,2048]{1,0:T(8,128)(2,1)} %get-tuple-element.178), channel_id=1, source_target_pairs={{16,4},{20,8},{24,12},{28,0},{17,5},{21,9},{25,13},{29,1},{18,6},{... | collective-permute-start | bytes 1572872 | tf_op jit(solution)/shard_map/ppermute | solution.py:499
  194.1 84.3 %collective-permute-start.16 = (bf16[128,2048]{1,0:T(8,128)(2,1)}, bf16[128,2048]{1,0:T(8,128)(2,1)}, u32[]{:S(2)}, u32[]{:S(2)}) collective-permute-start(bf16[128,2048]{1,0:T(8,128)(2,1)} %get-tuple-element.179), channel_id=1, source_target_pairs={{16,8},{20,12},{24,0},{28,4},{17,9},{21,13},{25,1},{29,5},{18,10},... | collective-permute-start | bytes 1572872 | tf_op jit(solution)/shard_map/ppermute | solution.py:499
  195.5 90.7 %collective-permute-start.17 = (bf16[128,2048]{1,0:T(8,128)(2,1)}, bf16[128,2048]{1,0:T(8,128)(2,1)S(1)}, u32[]{:S(2)}, u32[]{:S(2)}) collective-permute-start(bf16[128,2048]{1,0:T(8,128)(2,1)} %get-tuple-element.180), channel_id=1, source_target_pairs={{16,12},{20,0},{24,4},{28,8},{17,13},{21,1},{25,5},{29,9},{18,14},... | collective-permute-start | bytes 1572872 | tf_op jit(solution)/shard_map/ppermute | solution.py:499
  252.8 70.3 %collective-permute-start.21 = (bf16[128,2048]{1,0:T(8,128)(2,1)}, bf16[128,2048]{1,0:T(8,128)(2,1)S(1)}, u32[]{:S(2)}, u32[]{:S(2)}) collective-permute-start(bf16[128,2048]{1,0:T(8,128)(2,1)} %get-tuple-element.192), channel_id=1, source_target_pairs={{16,0},{20,4},{24,8},{28,12},{17,1},{21,5},{25,9},{29,13},{18,2},{... | collective-permute-start | bytes 1572872 | tf_op jit(solution)/shard_map/ppermute | solution.py:499
  254.4 102.2 %collective-permute-start.22 = (bf16[128,2048]{1,0:T(8,128)(2,1)}, bf16[128,2048]{1,0:T(8,128)(2,1)S(1)}, u32[]{:S(2)}, u32[]{:S(2)}) collective-permute-start(bf16[128,2048]{1,0:T(8,128)(2,1)} %get-tuple-element.193), channel_id=1, source_target_pairs={{16,4},{20,8},{24,12},{28,0},{17,5},{21,9},{25,13},{29,1},{18,6},{... | collective-permute-start | bytes 1572872 | tf_op jit(solution)/shard_map/ppermute | solution.py:499
  256.6 101.8 %collective-permute-start.23 = (bf16[128,2048]{1,0:T(8,128)(2,1)}, bf16[128,2048]{1,0:T(8,128)(2,1)S(1)}, u32[]{:S(2)}, u32[]{:S(2)}) collective-permute-start(bf16[128,2048]{1,0:T(8,128)(2,1)} %get-tuple-element.194), channel_id=1, source_target_pairs={{16,8},{20,12},{24,0},{28,4},{17,9},{21,13},{25,1},{29,5},{18,10},... | collective-permute-start | bytes 1572872 | tf_op jit(solution)/shard_map/ppermute | solution.py:499
  278.5 80.0 %collective-permute-start.24 = (bf16[128,2048]{1,0:T(8,128)(2,1)}, bf16[128,2048]{1,0:T(8,128)(2,1)S(1)}, u32[]{:S(2)}, u32[]{:S(2)}) collective-permute-start(bf16[128,2048]{1,0:T(8,128)(2,1)} %get-tuple-element.195), channel_id=1, source_target_pairs={{16,12},{20,0},{24,4},{28,8},{17,13},{21,1},{25,5},{29,9},{18,14},... | collective-permute-start | bytes 1572872 | tf_op jit(solution)/shard_map/ppermute | solution.py:499
  288.2 87.9 %collective-permute-start.18 = (bf16[128,2048]{1,0:T(8,128)(2,1)S(1)}, bf16[128,2048]{1,0:T(8,128)(2,1)S(1)}, u32[]{:S(2)}, u32[]{:S(2)}) collective-permute-start(bf16[128,2048]{1,0:T(8,128)(2,1)S(1)} %get-tuple-element.297), channel_id=1, source_target_pairs={{0,4},{4,8},{8,12},{12,0},{1,5},{5,9},{9,13},{13,1},{2,6},{6,10},{... | collective-permute-start | bytes 1572872 | tf_op jit(solution)/shard_map/ppermute | solution.py:522
  323.1 66.3 %collective-permute-start.19 = (bf16[128,2048]{1,0:T(8,128)(2,1)S(1)}, bf16[128,2048]{1,0:T(8,128)(2,1)S(1)}, u32[]{:S(2)}, u32[]{:S(2)}) collective-permute-start(bf16[128,2048]{1,0:T(8,128)(2,1)S(1)} %get-tuple-element.297), channel_id=1, source_target_pairs={{0,8},{4,12},{8,0},{12,4},{1,9},{5,13},{9,1},{13,5},{2,10},{6,14},... | collective-permute-start | bytes 1572872 | tf_op jit(solution)/shard_map/ppermute | solution.py:522
  361.4 64.8 %collective-permute-start.25 = (bf16[128,2048]{1,0:T(8,128)(2,1)}, bf16[128,2048]{1,0:T(8,128)(2,1)S(1)}, u32[]{:S(2)}, u32[]{:S(2)}) collective-permute-start(bf16[128,2048]{1,0:T(8,128)(2,1)} %get-tuple-element.299), channel_id=1, source_target_pairs={{0,4},{4,8},{8,12},{12,0},{1,5},{5,9},{9,13},{13,1},{2,6},{6,10},{... | collective-permute-start | bytes 1572872 | tf_op jit(solution)/shard_map/ppermute | solution.py:522
  365.4 61.7 %collective-permute-start.26 = (bf16[128,2048]{1,0:T(8,128)(2,1)}, bf16[128,2048]{1,0:T(8,128)(2,1)S(1)}, u32[]{:S(2)}, u32[]{:S(2)}) collective-permute-start(bf16[128,2048]{1,0:T(8,128)(2,1)} %get-tuple-element.299), channel_id=1, source_target_pairs={{0,8},{4,12},{8,0},{12,4},{1,9},{5,13},{9,1},{13,5},{2,10},{6,14},... | collective-permute-start | bytes 1572872 | tf_op jit(solution)/shard_map/ppermute | solution.py:522
  442.7 64.9 %collective-permute-start.30 = (bf16[128,2048]{1,0:T(8,128)(2,1)}, bf16[128,2048]{1,0:T(8,128)(2,1)}, u32[]{:S(2)}, u32[]{:S(2)}) collective-permute-start(bf16[128,2048]{1,0:T(8,128)(2,1)} %get-tuple-element.217), channel_id=1, source_target_pairs={{0,4},{4,8},{8,12},{12,0},{1,5},{5,9},{9,13},{13,1},{2,6},{6,10},{... | collective-permute-start | bytes 1572872 | tf_op jit(solution)/shard_map/ppermute | solution.py:506
  504.4 93.4 %collective-permute-start.38 = (bf16[128,2048]{1,0:T(8,128)(2,1)}, bf16[128,2048]{1,0:T(8,128)(2,1)}, u32[]{:S(2)}, u32[]{:S(2)}) collective-permute-start(bf16[128,2048]{1,0:T(8,128)(2,1)} %get-tuple-element.239), channel_id=1, source_target_pairs={{0,4},{4,8},{8,12},{12,0},{1,5},{5,9},{9,13},{13,1},{2,6},{6,10},{... | collective-permute-start | bytes 1572872 | tf_op jit(solution)/shard_map/ppermute | solution.py:506
  520.7 62.6 %collective-permute-start.36 = (bf16[512,2048]{1,0:T(8,128)(2,1)}, bf16[512,2048]{1,0:T(8,128)(2,1)}, u32[]{:S(2)}, u32[]{:S(2)}) collective-permute-start(bf16[512,2048]{1,0:T(8,128)(2,1)} %select_convert_fusion.2), channel_id=1, source_target_pairs={{0,1},{1,0},{2,3},{3,2},{4,5},{5,4},{6,7},{7,6},{8,9},{9,8},{10,11... | collective-permute-start | bytes 6291464 | tf_op jit(solution)/shard_map/ppermute | solution.py:603
  525.5 67.1 %collective-permute-start.37 = (bf16[512,1536]{1,0:T(8,128)(2,1)}, bf16[512,1536]{1,0:T(8,128)(2,1)}, u32[]{:S(2)}, u32[]{:S(2)}) collective-permute-start(bf16[512,1536]{1,0:T(8,128)(2,1)} %fusion.2), channel_id=1, source_target_pairs={{0,1},{1,0},{2,3},{3,2},{4,5},{5,4},{6,7},{7,6},{8,9},{9,8},{10,11... | collective-permute-start | bytes 4718600 | tf_op jit(solution)/shard_map/ppermute | solution.py:603
  583.3 78.9 %collective-permute-start.55 = (bf16[512,512]{1,0:T(8,128)(2,1)}, bf16[512,512]{1,0:T(8,128)(2,1)}, u32[]{:S(2)}, u32[]{:S(2)}) collective-permute-start(bf16[512,512]{1,0:T(8,128)(2,1)} %add_convert_fusion.4), channel_id=1, source_target_pairs={{0,2},{1,3},{2,0},{3,1},{4,6},{5,7},{6,4},{7,5},{8,10},{9,11},{10,... | collective-permute-start | bytes 1572872 | tf_op jit(solution)/shard_map/ppermute | solution.py:612
  668.7 87.0 %collective-permute-start.57 = (bf16[2048,512]{1,0:T(8,128)(2,1)}, bf16[2048,512]{1,0:T(8,128)(2,1)S(1)}, u32[]{:S(2)}, u32[]{:S(2)}) collective-permute-start(bf16[2048,512]{1,0:T(8,128)(2,1)} %add_convert_fusion.1), channel_id=1, source_target_pairs={{0,2},{1,3},{2,0},{3,1},{4,6},{5,7},{6,4},{7,5},{8,10},{9,11},{10,... | collective-permute-start | bytes 6291464 | tf_op jit(solution)/shard_map/ppermute | solution.py:612
  669.2 86.4 %collective-permute-start.44 = (bf16[2048,512]{1,0:T(8,128)(2,1)}, bf16[2048,512]{1,0:T(8,128)(2,1)S(1)}, u32[]{:S(2)}, u32[]{:S(2)}) collective-permute-start(bf16[2048,512]{1,0:T(8,128)(2,1)} %select_convert_fusion.1), channel_id=1, source_target_pairs={{0,1},{1,0},{2,3},{3,2},{4,5},{5,4},{6,7},{7,6},{8,9},{9,8},{10,11... | collective-permute-start | bytes 6291464 | tf_op jit(solution)/shard_map/ppermute | solution.py:603
  675.5 83.0 %collective-permute-start.48 = (f32[1,3456]{1,0:T(1,128)S(1)}, f32[1,3456]{1,0:T(1,128)S(1)}, u32[]{:S(2)}, u32[]{:S(2)}) collective-permute-start(f32[1,3456]{1,0:T(1,128)S(1)} %get-tuple-element.308), channel_id=1, source_target_pairs={{0,1},{1,2},{2,3},{3,0},{4,5},{5,6},{6,7},{7,4},{8,9},{9,10},{10,1... | collective-permute-start | bytes 41480 | tf_op jit(solution)/shard_map/ppermute | solution.py:657
  679.5 79.1 %collective-permute-start.49 = (f32[1,3456]{1,0:T(1,128)S(1)}, f32[1,3456]{1,0:T(1,128)S(1)}, u32[]{:S(2)}, u32[]{:S(2)}) collective-permute-start(f32[1,3456]{1,0:T(1,128)S(1)} %get-tuple-element.310), channel_id=1, source_target_pairs={{0,2},{1,3},{2,0},{3,1},{4,6},{5,7},{6,4},{7,5},{8,10},{9,11},{10,... | collective-permute-start | bytes 41480 | tf_op jit(solution)/shard_map/ppermute | solution.py:657
  (76 other events, 1574.2 us)
